TPU v7x, 32 devices: a whole 2x2x4 slice. The times are simulated.
32 devices in a mesh: mem: 16 (over z, x, core), space: 2 (over y).
Axes of the slice: x: 2, y: 2, z: 4, core: 2. Of those that a mesh axis runs over, the one named last changes fastest.
Arguments:
- prior_samples: bfloat16 [256, 32, 4096], P('mem', 'space'), may hold values from -6 to 6
- diffusivity_field: float32 [32, 4096], P('space'), may hold values from 0.05 to 0.24
- measured_site_position: int32 [2, 16, 512], P('space', 'mem'), may hold values from 0 to 4095
- measured_quantities: float32 [2, 16, 512], P('space', 'mem'), may hold values from -6 to 6
- measurement_weightings: float32 [2, 16, 512], P('space', 'mem'), may hold values from 0.5 to 8
Outputs:
- analysis: bfloat16 [256, 32, 4096], P('mem', 'space')
Inputs may be any that keep to these rules, and one draw needn't show every extreme that they name: measured_site_position[p, q, o] names cell a * 256 + b of patch (p, q) itself.
All inputs are finite; a program needn't handle non-finite values.
Results may differ from a plain program's by a relative error of at most 0.0077.
Values may be sent and summed in bfloat16 or wider, within the bound.
A program may use at most 64 MiB of HBM per device.

v0:
```python
import jax
import jax.numpy as jnp
from jax import lax
from jax.sharding import PartitionSpec as P

ITERS = 10


HIGHEST = lax.Precision.HIGHEST


def padded_2(block, sides, width):
    for axis, dim in sides:
        count = lax.axis_size(axis)
        forward = [(i, i + 1) for i in range(count - 1)]
        backward = [(target, source) for source, target in forward]
        low = lax.ppermute(
            lax.slice_in_dim(block, block.shape[dim] - width, None, axis=dim), axis, forward
        )
        high = lax.ppermute(lax.slice_in_dim(block, 0, width, axis=dim), axis, backward)
        block = jnp.concatenate([low, block, high], axis=dim)
    return block


def interior(extended):
    middle = extended[:, 1:-1]
    padded = jnp.pad(middle, ((0, 0), (0, 0), (1, 1)))
    return extended[:, 2:] + extended[:, :-2] + padded[:, :, 2:] + padded[:, :, :-2] - 4.0 * middle


def body(
    prior_samples,
    diffusivity_field,
    measured_site_position,
    measured_quantities,
    measurement_weightings,
):
    present_sample = prior_samples.astype(jnp.float32)
    for repeat in range(2):
        extended = padded_2(present_sample, (("space", 1),), 1)
        present_sample = present_sample + diffusivity_field[None] * interior(extended)
    advanced_sample = present_sample.astype(jnp.bfloat16)
    patch_cells = lax.all_to_all(advanced_sample, "mem", split_axis=2, concat_axis=0, tiled=True)
    members, rows_a, rows_b = patch_cells.shape
    patch_rows = patch_cells.reshape(members, rows_a * rows_b)
    observed = jnp.take(patch_rows, measured_site_position[0, 0], axis=1).astype(jnp.float32)
    obs_mean = jnp.mean(observed, axis=0)
    obs_root = jnp.sqrt(measurement_weightings[0, 0])
    spread = ((observed - obs_mean[None, :]) * obs_root[None, :]).astype(jnp.bfloat16)
    innovation = ((measured_quantities[0, 0] - obs_mean) * obs_root).astype(jnp.bfloat16)
    own_gram = lax.dot_general(
        spread, spread, (((1,), (1,)), ((), ())), preferred_element_type=jnp.float32
    )
    own_vector = jnp.dot(spread, innovation, preferred_element_type=jnp.float32)
    side_grams, side_vectors = (
        padded_2(own_gram[None], (("mem", 0),), 1),
        padded_2(own_vector[None], (("mem", 0),), 1),
    )
    band_gram = 0.5 * side_grams[0] + side_grams[1] + 0.5 * side_grams[2]
    band_vector = 0.5 * side_vectors[0] + side_vectors[1] + 0.5 * side_vectors[2]
    upper_grams, upper_vectors = (
        padded_2(band_gram[None], (("space", 0),), 1),
        padded_2(band_vector[None], (("space", 0),), 1),
    )
    gram = 0.5 * upper_grams[0] + upper_grams[1] + 0.5 * upper_grams[2]
    vector = 0.5 * upper_vectors[0] + upper_vectors[1] + 0.5 * upper_vectors[2]
    identity = jnp.eye(members, dtype=jnp.float32)
    system = gram + (members - 1.0) * identity
    frobenius = jnp.sqrt(jnp.sum(system * system))

    def newton(counter, pair):
        root_part, inverse_part = pair
        factor = 1.5 * identity - 0.5 * jnp.dot(inverse_part, root_part, precision=HIGHEST)
        return (
            jnp.dot(root_part, factor, precision=HIGHEST),
            jnp.dot(factor, inverse_part, precision=HIGHEST),
        )

    root_part, inverse_part = lax.fori_loop(0, ITERS, newton, (system / frobenius, identity))
    inverse_root = inverse_part / jnp.sqrt(frobenius)
    mean_weights = jnp.dot(
        inverse_root, jnp.dot(inverse_root, vector, precision=HIGHEST), precision=HIGHEST
    )
    transform = (jnp.sqrt(members - 1.0) * inverse_root + mean_weights[:, None]).astype(
        jnp.bfloat16
    )
    state_mean = jnp.mean(patch_rows, axis=0, dtype=jnp.float32)
    deviation = (patch_rows.astype(jnp.float32) - state_mean[None, :]).astype(jnp.bfloat16)
    moved = lax.dot_general(
        transform, deviation, (((0,), (0,)), ((), ())), preferred_element_type=jnp.float32
    )
    updated = (state_mean[None, :] + moved).astype(jnp.bfloat16).reshape(members, rows_a, rows_b)
    returned = lax.all_to_all(updated, "mem", split_axis=0, concat_axis=2, tiled=True)
    extended = padded_2(returned, (("space", 1),), 1).astype(jnp.float32)
    return (returned.astype(jnp.float32) + diffusivity_field[None] * interior(extended)).astype(
        jnp.bfloat16
    )


def solution(mesh):
    return jax.shard_map(
        body,
        mesh=mesh,
        in_specs=(
            P("mem", "space", None),
            P("space", None),
            P("space", "mem", None),
            P("space", "mem", None),
            P("space", "mem", None),
        ),
        out_specs=P("mem", "space", None),
        check_vma=False,
    )
```

profile of v0, /device:TPU:0, one launch (start us, length us, event | category | flops | bytes accessed | tf_op | source)
XLA Modules:
  0.0 286.1 jit_solution(7173300072680920156)
XLA Ops:
  0.0 2.9 copy_convert_fusion
  4.2 4.9 %collective-permute-start.1 = (f32[16,1,4096]{2,0,1:T(8,128)S(1)}, f32[16,1,4096]{2,0,1:T(8,128)S(1)}, u32[]{:S(2)}, u32[]{:S(2)}) collective-permute-start(f32[16,1,4096]{2,0,1:T(8,128)S(1)} %get-tuple-element.56), channel_id=1, source_target_pairs={{0,1},{2,3},{4,5},{6,7},{8,9},{10,11},{12,13},{14,15},{16,17},{18,... | collective-permute-start | bytes 786440 | tf_op jit(solution)/shard_map/ppermute | solution.py:17
  9.1 4.4 %collective-permute-done = f32[16,1,4096]{2,0,1:T(8,128)S(1)} collective-permute-done((f32[16,1,4096]{2,0,1:T(8,128)S(1)}, f32[16,1,4096]{2,0,1:T(8,128)S(1)}, u32[]{:S(2)}, u32[]{:S(2)}) %collective-permute-start) | collective-permute-done | bytes 262176 | tf_op jit(solution)/shard_map/ppermute | solution.py:20
  14.7 2.7 fusion.22
  18.8 4.6 %collective-permute-start.3 = (f32[16,1,4096]{2,0,1:T(8,128)S(1)}, f32[16,1,4096]{2,0,1:T(8,128)S(1)}, u32[]{:S(2)}, u32[]{:S(2)}) collective-permute-start(f32[16,1,4096]{2,0,1:T(8,128)S(1)} %get-tuple-element.54), channel_id=1, source_target_pairs={{0,1},{2,3},{4,5},{6,7},{8,9},{10,11},{12,13},{14,15},{16,17},{18,... | collective-permute-start | bytes 786440 | tf_op jit(solution)/shard_map/ppermute | solution.py:17
  23.3 3.3 %collective-permute-done.2 = f32[16,1,4096]{2,0,1:T(8,128)S(1)} collective-permute-done((f32[16,1,4096]{2,0,1:T(8,128)S(1)}, f32[16,1,4096]{2,0,1:T(8,128)S(1)}, u32[]{:S(2)}, u32[]{:S(2)}) %collective-permute-start.2) | collective-permute-done | bytes 262176 | tf_op jit(solution)/shard_map/ppermute | solution.py:20
  27.9 2.8 fusion.16
  30.7 14.3 %copy.15 = bf16[16,16,4096]{1,0,2:T(8,128)(2,1)} copy(bf16[16,16,4096]{2,0,1:T(8,128)(2,1)S(1)} %fusion.16) | data formatting | bytes 4194304 | tf_op jit(solution)/shard_map/convert_element_type | solution.py:42
  45.0 20.8 %reshape.93 = bf16[16,2,32768]{2,1,0:T(2,128)(2,1)} reshape(bf16[4096,16,16]{2,1,0:T(8,128)(2,1)} %bitcast.97) | data formatting | bytes 4194304
  65.8 6.6 %all-to-all-start = ((bf16[16,2,32768]{2,1,0:T(2,128)(2,1)}), bf16[16,2,32768]{2,1,0:T(2,128)(2,1)S(1)}, u32[]{:S(2)}, u32[]{:S(2)}) async-start(bf16[16,2,32768]{2,1,0:T(2,128)(2,1)} %reshape.93), calls=%async_computation | async-start | bytes 4194304 | tf_op jit(solution)/shard_map/all_to_all | solution.py:43
  72.5 40.9 %all-to-all-done = bf16[16,2,32768]{2,1,0:T(2,128)(2,1)S(1)} async-done(((bf16[16,2,32768]{2,1,0:T(2,128)(2,1)}), bf16[16,2,32768]{2,1,0:T(2,128)(2,1)S(1)}, u32[]{:S(2)}, u32[]{:S(2)}) %all-to-all-start) | async-done | bytes 2097184 | tf_op jit(solution)/shard_map/all_to_all | solution.py:43
  113.3 14.3 %reshape.94 = bf16[4096,16,16]{2,1,0:T(8,128)(2,1)} reshape(bf16[16,2,32768]{2,1,0:T(2,128)(2,1)S(1)} %all-to-all-done) | data formatting | bytes 4194304
  127.6 16.9 %copy.16 = bf16[16,16,16,256]{3,1,0,2:T(8,128)(2,1)S(1)} copy(bf16[16,16,16,256]{1,0,3,2:T(8,128)(2,1)} %bitcast.98) | data formatting | bytes 4194304 | tf_op jit(solution)/shard_map/all_to_all | solution.py:43
  144.6 2.2 copy.22
  146.8 4.1 %copy.17 = bf16[256,4096]{0,1:T(8,128)(2,1)} copy(bf16[256,4096]{1,0:T(8,128)(2,1)} %bitcast.100) | data formatting | bytes 4194304 | tf_op jit(solution)/shard_map/reshape | solution.py:45
  150.9 3.4 %gather_fusion = bf16[512,256]{1,0:T(8,128)(2,1)S(1)} fusion(bf16[256,4096]{0,1:T(8,128)(2,1)} %copy.17, s32[1024]{0:T(1024)S(1)} %pad_clamp_fusion), kind=kCustom, calls=%fused_computation | custom fusion | bytes 526336 | tf_op jit(solution)/shard_map/jit(_take)/gather | solution.py:46
  155.1 2.9 %collective-permute-start.4 = (f32[1,256,256]{2,1,0:T(8,128)S(1)}, f32[1,256,256]{2,1,0:T(8,128)S(1)}, u32[]{:S(2)}, u32[]{:S(2)}) collective-permute-start(f32[1,256,256]{2,1,0:T(8,128)S(1)} %bitcast.105), channel_id=1, source_target_pairs={{0,2},{2,4},{4,6},{6,8},{8,10},{10,12},{12,14},{14,16},{16,18},{18... | collective-permute-start | bytes 786440 | tf_op jit(solution)/shard_map/ppermute | solution.py:17
  159.5 5.0 %collective-permute-start.8 = (f32[1,256]{1,0:T(1,128)S(1)}, f32[1,256]{1,0:T(1,128)S(1)}, u32[]{:S(2)}, u32[]{:S(2)}) collective-permute-start(f32[1,256]{1,0:T(1,128)S(1)} %fusion.26), channel_id=1, source_target_pairs={{0,2},{2,4},{4,6},{6,8},{8,10},{10,12},{12,14},{14,16},{16,18},{18... | collective-permute-start | bytes 3080 | tf_op jit(solution)/shard_map/ppermute | solution.py:17
  166.2 2.6 collective-permute-done.9
  168.8 4.4 %collective-permute-start.10 = (f32[1,256]{1,0:T(1,128)S(1)}, f32[1,256]{1,0:T(1,128)S(1)}, u32[]{:S(2)}, u32[]{:S(2)}) collective-permute-start(f32[1,256]{1,0:T(1,128)S(1)} %bitcast.118), channel_id=1, source_target_pairs={{0,1},{2,3},{4,5},{6,7},{8,9},{10,11},{12,13},{14,15},{16,17},{18,... | collective-permute-start | bytes 3080 | tf_op jit(solution)/shard_map/ppermute | solution.py:17
  174.7 4.6 %collective-permute-start.6 = (f32[1,256,256]{2,1,0:T(8,128)S(1)}, f32[1,256,256]{2,1,0:T(8,128)S(1)}, u32[]{:S(2)}, u32[]{:S(2)}) collective-permute-start(f32[1,256,256]{2,1,0:T(8,128)S(1)} %fusion.34), channel_id=1, source_target_pairs={{0,1},{2,3},{4,5},{6,7},{8,9},{10,11},{12,13},{14,15},{16,17},{18,... | collective-permute-start | bytes 786440 | tf_op jit(solution)/shard_map/ppermute | solution.py:17
  180.7 2.8 collective-permute-done.6
  183.5 4.7 %collective-permute-done.7 = f32[1,256,256]{2,1,0:T(8,128)S(1)} collective-permute-done((f32[1,256,256]{2,1,0:T(8,128)S(1)}, f32[1,256,256]{2,1,0:T(8,128)S(1)}, u32[]{:S(2)}, u32[]{:S(2)}) %collective-permute-start.7) | collective-permute-done | bytes 262176 | tf_op jit(solution)/shard_map/ppermute | solution.py:20
  190.0 14.8 %while.13 = (s32[]{:T(128)}, f32[256,256]{0,1:T(8,128)S(1)}, f32[256,256]{1,0:T(8,128)S(1)}, s32[]{:T(128)}) while((s32[]{:T(128)}, f32[256,256]{0,1:T(8,128)S(1)}, f32[256,256]{1,0:T(8,128)S(1)}, s32[]{:T(128)}) %tuple.29), condition=%wide.region_4.5_spmd.clone, body=%wide.region_3.4_spmd.clone.sunk | while | flops 604241920 | bytes 3407925 | solution.py:79
  207.0 58.3 %all_to_all.33 = bf16[256,16,256]{2,1,0:T(8,128)(2,1)S(1)} all-to-all(bf16[256,16,256]{2,1,0:T(8,128)(2,1)S(1)} %bitcast.102), channel_id=1, replica_groups=mesh['mem'=16,'space'=2] {'mem'}, dimensions={0} | all-to-all | bytes 4194304 | tf_op jit(solution)/shard_map/all_to_all | solution.py:93
  265.2 2.5 copy.26
  267.7 2.9 %all_to_all.30 = bf16[16,16,4096]{2,0,1:T(8,128)(2,1)S(1)} reshape(bf16[16,16,16,256]{3,2,0,1:T(8,128)(2,1)} %bitcast.104) | data formatting | bytes 4194304 | tf_op jit(solution)/shard_map/all_to_all | solution.py:93
  270.7 1.7 collective-permute-start.12
  273.7 2.6 collective-permute-done.12
  276.3 4.1 %collective-permute-done.13 = bf16[16,1,4096]{2,0,1:T(8,128)(2,1)S(1)} collective-permute-done((bf16[16,1,4096]{2,0,1:T(8,128)(2,1)S(1)}, bf16[16,1,4096]{2,0,1:T(8,128)(2,1)S(1)}, u32[]{:S(2)}, u32[]{:S(2)}) %collective-permute-start.13) | collective-permute-done | bytes 131104 | tf_op jit(solution)/shard_map/ppermute | solution.py:20
  281.2 2.4 fusion.9
  283.6 2.5 copy.20
  (107 shorter events, 31.3 us)
Async XLA Ops:
  0.0 14.7 %copy-start.1 = (f32[16,4096]{1,0:T(8,128)S(1)}, f32[16,4096]{1,0:T(8,128)}, u32[]{:S(2)}) copy-start(f32[16,4096]{1,0:T(8,128)} %param.8) | copy-start | bytes 786436
  2.9 10.6 %collective-permute-start = (f32[16,1,4096]{2,0,1:T(8,128)S(1)}, f32[16,1,4096]{2,0,1:T(8,128)S(1)}, u32[]{:S(2)}, u32[]{:S(2)}) collective-permute-start(f32[16,1,4096]{2,0,1:T(8,128)S(1)} %get-tuple-element.55), channel_id=1, source_target_pairs={{1,0},{3,2},{5,4},{7,6},{9,8},{11,10},{13,12},{15,14},{17,16},{19,... | collective-permute-start | bytes 786440 | tf_op jit(solution)/shard_map/ppermute | solution.py:20
  4.2 10.5 %collective-permute-start.1 = (f32[16,1,4096]{2,0,1:T(8,128)S(1)}, f32[16,1,4096]{2,0,1:T(8,128)S(1)}, u32[]{:S(2)}, u32[]{:S(2)}) collective-permute-start(f32[16,1,4096]{2,0,1:T(8,128)S(1)} %get-tuple-element.56), channel_id=1, source_target_pairs={{0,1},{2,3},{4,5},{6,7},{8,9},{10,11},{12,13},{14,15},{16,17},{18,... | collective-permute-start | bytes 786440 | tf_op jit(solution)/shard_map/ppermute | solution.py:17
  17.5 9.2 %collective-permute-start.2 = (f32[16,1,4096]{2,0,1:T(8,128)S(1)}, f32[16,1,4096]{2,0,1:T(8,128)S(1)}, u32[]{:S(2)}, u32[]{:S(2)}) collective-permute-start(f32[16,1,4096]{2,0,1:T(8,128)S(1)} %get-tuple-element.53), channel_id=1, source_target_pairs={{1,0},{3,2},{5,4},{7,6},{9,8},{11,10},{13,12},{15,14},{17,16},{19,... | collective-permute-start | bytes 786440 | tf_op jit(solution)/shard_map/ppermute | solution.py:20
  18.8 9.1 %collective-permute-start.3 = (f32[16,1,4096]{2,0,1:T(8,128)S(1)}, f32[16,1,4096]{2,0,1:T(8,128)S(1)}, u32[]{:S(2)}, u32[]{:S(2)}) collective-permute-start(f32[16,1,4096]{2,0,1:T(8,128)S(1)} %get-tuple-element.54), channel_id=1, source_target_pairs={{0,1},{2,3},{4,5},{6,7},{8,9},{10,11},{12,13},{14,15},{16,17},{18,... | collective-permute-start | bytes 786440 | tf_op jit(solution)/shard_map/ppermute | solution.py:17
  65.8 6.6 %copy-start.3 = (f32[1,1,512]{2,1,0:T(1,128)S(1)}, f32[1,1,512]{2,1,0:T(1,128)}, u32[]{:S(2)}) copy-start(f32[1,1,512]{2,1,0:T(1,128)} %param.11) | copy-start | bytes 6148
  65.8 6.6 %copy-start.2 = (s32[1,1,512]{2,1,0:T(1,128)S(1)}, s32[1,1,512]{2,1,0:T(1,128)}, u32[]{:S(2)}) copy-start(s32[1,1,512]{2,1,0:T(1,128)} %param.9) | copy-start | bytes 6148
  65.8 47.5 %all-to-all-start = ((bf16[16,2,32768]{2,1,0:T(2,128)(2,1)}), bf16[16,2,32768]{2,1,0:T(2,128)(2,1)S(1)}, u32[]{:S(2)}, u32[]{:S(2)}) async-start(bf16[16,2,32768]{2,1,0:T(2,128)(2,1)} %reshape.93), calls=%async_computation | async-start | bytes 4194304 | tf_op jit(solution)/shard_map/all_to_all | solution.py:43
  146.8 7.8 %copy-start.4 = (f32[1,1,512]{2,1,0:T(1,128)S(1)}, f32[1,1,512]{2,1,0:T(1,128)}, u32[]{:S(2)}) copy-start(f32[1,1,512]{2,1,0:T(1,128)} %param.10) | copy-start | bytes 6148
  155.1 19.4 %collective-permute-start.4 = (f32[1,256,256]{2,1,0:T(8,128)S(1)}, f32[1,256,256]{2,1,0:T(8,128)S(1)}, u32[]{:S(2)}, u32[]{:S(2)}) collective-permute-start(f32[1,256,256]{2,1,0:T(8,128)S(1)} %bitcast.105), channel_id=1, source_target_pairs={{0,2},{2,4},{4,6},{6,8},{8,10},{10,12},{12,14},{14,16},{16,18},{18... | collective-permute-start | bytes 786440 | tf_op jit(solution)/shard_map/ppermute | solution.py:17
  158.0 16.6 %collective-permute-start.5 = (f32[1,256,256]{2,1,0:T(8,128)S(1)}, f32[1,256,256]{2,1,0:T(8,128)S(1)}, u32[]{:S(2)}, u32[]{:S(2)}) collective-permute-start(f32[1,256,256]{2,1,0:T(8,128)S(1)} %bitcast.106), channel_id=1, source_target_pairs={{2,0},{4,2},{6,4},{8,6},{10,8},{12,10},{14,12},{16,14},{18,16},{20... | collective-permute-start | bytes 786440 | tf_op jit(solution)/shard_map/ppermute | solution.py:20
  159.5 6.7 %collective-permute-start.8 = (f32[1,256]{1,0:T(1,128)S(1)}, f32[1,256]{1,0:T(1,128)S(1)}, u32[]{:S(2)}, u32[]{:S(2)}) collective-permute-start(f32[1,256]{1,0:T(1,128)S(1)} %fusion.26), channel_id=1, source_target_pairs={{0,2},{2,4},{4,6},{6,8},{8,10},{10,12},{12,14},{14,16},{16,18},{18... | collective-permute-start | bytes 3080 | tf_op jit(solution)/shard_map/ppermute | solution.py:17
  164.5 4.3 %collective-permute-start.9 = (f32[1,256]{1,0:T(1,128)S(1)}, f32[1,256]{1,0:T(1,128)S(1)}, u32[]{:S(2)}, u32[]{:S(2)}) collective-permute-start(f32[1,256]{1,0:T(1,128)S(1)} %fusion.26), channel_id=1, source_target_pairs={{2,0},{4,2},{6,4},{8,6},{10,8},{12,10},{14,12},{16,14},{18,16},{20... | collective-permute-start | bytes 3080 | tf_op jit(solution)/shard_map/ppermute | solution.py:20
  168.8 5.7 %collective-permute-start.10 = (f32[1,256]{1,0:T(1,128)S(1)}, f32[1,256]{1,0:T(1,128)S(1)}, u32[]{:S(2)}, u32[]{:S(2)}) collective-permute-start(f32[1,256]{1,0:T(1,128)S(1)} %bitcast.118), channel_id=1, source_target_pairs={{0,1},{2,3},{4,5},{6,7},{8,9},{10,11},{12,13},{14,15},{16,17},{18,... | collective-permute-start | bytes 3080 | tf_op jit(solution)/shard_map/ppermute | solution.py:17
  173.2 7.5 %collective-permute-start.11 = (f32[1,256]{1,0:T(1,128)S(1)}, f32[1,256]{1,0:T(1,128)S(1)}, u32[]{:S(2)}, u32[]{:S(2)}) collective-permute-start(f32[1,256]{1,0:T(1,128)S(1)} %bitcast.119), channel_id=1, source_target_pairs={{1,0},{3,2},{5,4},{7,6},{9,8},{11,10},{13,12},{15,14},{17,16},{19,... | collective-permute-start | bytes 3080 | tf_op jit(solution)/shard_map/ppermute | solution.py:20
  174.7 8.9 %collective-permute-start.6 = (f32[1,256,256]{2,1,0:T(8,128)S(1)}, f32[1,256,256]{2,1,0:T(8,128)S(1)}, u32[]{:S(2)}, u32[]{:S(2)}) collective-permute-start(f32[1,256,256]{2,1,0:T(8,128)S(1)} %fusion.34), channel_id=1, source_target_pairs={{0,1},{2,3},{4,5},{6,7},{8,9},{10,11},{12,13},{14,15},{16,17},{18,... | collective-permute-start | bytes 786440 | tf_op jit(solution)/shard_map/ppermute | solution.py:17
  179.2 9.0 %collective-permute-start.7 = (f32[1,256,256]{2,1,0:T(8,128)S(1)}, f32[1,256,256]{2,1,0:T(8,128)S(1)}, u32[]{:S(2)}, u32[]{:S(2)}) collective-permute-start(f32[1,256,256]{2,1,0:T(8,128)S(1)} %fusion.34), channel_id=1, source_target_pairs={{1,0},{3,2},{5,4},{7,6},{9,8},{11,10},{13,12},{15,14},{17,16},{19,... | collective-permute-start | bytes 786440 | tf_op jit(solution)/shard_map/ppermute | solution.py:20
  190.0 15.4 %copy-start = (bf16[32,8,16,256]{3,1,2,0:T(8,128)(2,1)S(1)}, bf16[32,8,16,256]{3,1,2,0:T(8,128)(2,1)}, u32[]{:S(2)}) copy-start(bf16[32,8,16,256]{3,1,2,0:T(8,128)(2,1)} %copy.22) | copy-start | bytes 6291460
  270.7 5.6 %collective-permute-start.12 = (bf16[16,1,4096]{2,0,1:T(8,128)(2,1)S(1)}, bf16[16,1,4096]{2,0,1:T(8,128)(2,1)S(1)}, u32[]{:S(2)}, u32[]{:S(2)}) collective-permute-start(bf16[16,1,4096]{2,0,1:T(8,128)(2,1)S(1)} %get-tuple-element.57), channel_id=1, source_target_pairs={{0,1},{2,3},{4,5},{6,7},{8,9},{10,11},{12,13},{14,15},{16,17},{18,... | collective-permute-start | bytes 393224 | tf_op jit(solution)/shard_map/ppermute | solution.py:17
  272.4 8.0 %collective-permute-start.13 = (bf16[16,1,4096]{2,0,1:T(8,128)(2,1)S(1)}, bf16[16,1,4096]{2,0,1:T(8,128)(2,1)S(1)}, u32[]{:S(2)}, u32[]{:S(2)}) collective-permute-start(bf16[16,1,4096]{2,0,1:T(8,128)(2,1)S(1)} %get-tuple-element.58), channel_id=1, source_target_pairs={{1,0},{3,2},{5,4},{7,6},{9,8},{11,10},{13,12},{15,14},{17,16},{19,... | collective-permute-start | bytes 393224 | tf_op jit(solution)/shard_map/ppermute | solution.py:20
where the time goes:
time: 288 us; the launch traced here: 286 us
  local copies, waits for them, and re-layouts  85.6 us (30%)
  waiting for transfers between devices  67.8 us (24%)
  blocking collectives  58.3 us (20%)
  starting transfers between devices  43.9 us (15%)
  matrix products  15.8 us (5%)
  other arithmetic  12.9 us (4%)
    all_to_all x1, blocking collectives, body(): lax.all_to_all(updated, 'mem', split_axis=0, concat_axis=2, tiled=True)  58.3 us
    all_to_all x1, waiting for transfers between devices, body(): lax.all_to_all(advanced_sample, 'mem', split_axis=2, concat_axis=0, tiled...  40.9 us
    unnamed x16, local copies, waits for them, and re-layouts  38.1 us
    ppermute x7, starting transfers between devices, padded_2(): lax.ppermute(lax.slice_in_dim(block, block.shape[dim] - width, None, axis...  28.1 us
    ppermute x7, waiting for transfers between devices, padded_2(): lax.ppermute(lax.slice_in_dim(block, 0, width, axis=dim), axis, backward)  19.2 us
    all_to_all x1, local copies, waits for them, and re-layouts, body(): lax.all_to_all(advanced_sample, 'mem', split_axis=2, concat_axis=0, tiled...  16.9 us
    convert_element_type x1, local copies, waits for them, and re-layouts, body(): advanced_sample = present_sample.astype(jnp.bfloat16)  14.3 us
    ppermute x7, starting transfers between devices, padded_2(): lax.ppermute(lax.slice_in_dim(block, 0, width, axis=dim), axis, backward)  9.23 us
  transfers between devices with their start and end apart: 15, of which 10 were waited for; matrix products, arithmetic and copies ran while one was open for 0% of the time, Pallas kernels for 0%

commit v1 on v0

v1 whole, which is shorter than its diff:
```python
import functools
import math

import jax
import jax.numpy as jnp
from jax import lax
from jax.experimental import pallas as pl
from jax.experimental.pallas import tpu as pltpu
from jax.sharding import PartitionSpec as P

ITERS = 10
PAD = 128
F32 = jnp.float32
BF16 = jnp.bfloat16
VMEM = pl.BlockSpec(memory_space=pltpu.VMEM)


def exchange(low_edge, high_edge, axis):
    count = lax.axis_size(axis)
    forward = [(i, i + 1) for i in range(count - 1)]
    backward = [(target, source) for source, target in forward]
    return lax.ppermute(high_edge, axis, forward), lax.ppermute(low_edge, axis, backward)


def swap_matrix(outer, inner):
    size = outer * inner
    row = lax.broadcasted_iota(jnp.int32, (size, size), 0)
    col = lax.broadcasted_iota(jnp.int32, (size, size), 1)
    return ((row % inner) * outer + row // inner == col).astype(BF16)


def merged(block):
    a, m, c = block.shape
    if m % 16 == 0:
        return block.reshape(a * m, c)
    return block.astype(F32).reshape(a * m, c).astype(BF16)


def halves(value):
    high = value.astype(BF16)
    return high, (value - high.astype(F32)).astype(BF16)


def dot1(a, b):
    return jnp.dot(a, b, preferred_element_type=F32)


def dot3(a, b):
    ah, al = a
    bh, bl = b
    return dot1(ah, bh) + (dot1(ah, bl) + dot1(al, bh))


def step_row(src, row, diffusion, width):
    mid = src[row, :, PAD : PAD + width]
    around = (
        src[row - 1, :, PAD : PAD + width]
        + src[row + 1, :, PAD : PAD + width]
        + src[row, :, PAD - 1 : PAD - 1 + width]
        + src[row, :, PAD + 1 : PAD + 1 + width]
    )
    return mid + diffusion * (around - 4.0 * mid)


def clear_pads(buf, width):
    rows, m, _ = buf.shape
    buf[:, :, :PAD] = jnp.zeros((rows, m, PAD), F32)
    buf[:, :, PAD + width :] = jnp.zeros((rows, m, PAD), F32)


def forecast_kernel(x_ref, swap_ref, d_ref, low_ref, high_ref, out_ref, xs, v1):
    patches, rows, m, cols = out_ref.shape
    width = patches * cols
    clear_pads(xs, width)
    clear_pads(v1, width)
    xs[0:2, :, PAD : PAD + width] = low_ref[...].astype(F32)
    xs[rows + 2 : rows + 4, :, PAD : PAD + width] = high_ref[...].astype(F32)

    @pl.loop(0, patches // 2)
    def _(c):
        at = pl.multiple_of(c * 2 * cols, 128)
        part = dot1(swap_ref[...], x_ref[:, pl.ds(at, 2 * cols)])
        xs[2 : rows + 2, :, pl.ds(at + PAD, 2 * cols)] = part.reshape(rows, m, 2 * cols)

    @pl.loop(1, rows + 3)
    def _(r):
        v1[r, :, PAD : PAD + width] = step_row(xs, r, d_ref[r - 1], width)

    @pl.loop(2, rows + 2)
    def _(r):
        fresh = step_row(v1, r, d_ref[r - 1], width).astype(BF16)
        for q in range(patches):
            out_ref[q, r - 2] = fresh[:, q * cols : (q + 1) * cols]


def observe_kernel(patch_ref, site_ref, value_ref, weight_ref, out_ref, acc):
    owners, rows, m, cols = patch_ref.shape
    members = owners * m
    obs = site_ref.shape[1]
    acc[...] = jnp.zeros_like(acc)

    @pl.loop(0, rows)
    def _(r):
        cell = lax.broadcasted_iota(jnp.int32, (cols, obs), 0) + r * cols
        picked = jnp.where(cell == site_ref[...], 1.0, 0.0).astype(BF16)
        acc[...] += dot1(merged(patch_ref[:, r]), picked)

    observed = acc[...]
    obs_mean = jnp.sum(observed, axis=0, keepdims=True) * (1.0 / members)
    root = jnp.sqrt(weight_ref[...])
    spread = ((observed - obs_mean) * root).astype(BF16)
    innovation = ((value_ref[...] - obs_mean) * root).astype(BF16)
    contract = (((1,), (1,)), ((), ()))
    out_ref[0:members, :] = lax.dot_general(spread, spread, contract, preferred_element_type=F32)
    wide = jnp.broadcast_to(innovation.astype(F32), (8, obs)).astype(BF16)
    out_ref[members : members + 8, :] = lax.dot_general(
        wide, spread, contract, preferred_element_type=F32
    )


def analyse_kernel(gram_ref, patch_ref, out_ref):
    owners, rows, m, cols = patch_ref.shape
    members = owners * m
    identity = (
        lax.broadcasted_iota(jnp.int32, (members, members), 0)
        == lax.broadcasted_iota(jnp.int32, (members, members), 1)
    ).astype(F32)
    system = gram_ref[0:members, :] + (members - 1.0) * identity
    vector = gram_ref[members : members + 8, :]
    frob = jnp.sqrt(jnp.sum(jnp.sum(system * system, axis=1, keepdims=True), axis=0, keepdims=True))
    root_part = system / frob
    factor = 1.5 * identity - 0.5 * root_part
    root_part = dot3(halves(root_part), halves(factor))
    inverse_part = factor
    for step in range(1, ITERS):
        r, z = halves(root_part), halves(inverse_part)
        f = halves(1.5 * identity - 0.5 * dot3(z, r))
        if step < ITERS - 1:
            root_part = dot3(r, f)
        inverse_part = dot3(f, z)
    inverse_root = inverse_part / jnp.sqrt(frob)
    z = halves(inverse_root)
    weights = dot3(halves(dot3(halves(vector), z)), z)[0:1, :]
    turned = (math.sqrt(members - 1.0) * inverse_root + weights).astype(BF16)

    @pl.loop(0, rows)
    def _(r):
        cells = merged(patch_ref[:, r]).astype(F32)
        mean = jnp.sum(cells, axis=0, keepdims=True) * (1.0 / members)
        updated = mean + dot1(turned, (cells - mean).astype(BF16))
        out_ref[:, r] = updated.reshape(owners, m, cols).astype(BF16)


def finish_kernel(x_ref, swap_ref, d_ref, low_ref, high_ref, out_ref, xs, moved):
    patches, rows, m, cols = x_ref.shape
    width = patches * cols
    clear_pads(xs, width)
    for q in range(patches):
        at = slice(PAD + q * cols, PAD + (q + 1) * cols)
        xs[0, :, at] = low_ref[q].astype(F32)
        xs[rows + 1, :, at] = high_ref[q].astype(F32)
        xs[1 : rows + 1, :, at] = x_ref[q].astype(F32)

    @pl.loop(1, rows + 1)
    def _(r):
        moved[r - 1] = step_row(xs, r, d_ref[r - 1], width).astype(BF16)

    @pl.loop(0, patches // 2)
    def _(c):
        at = pl.multiple_of(c * 2 * cols, 128)
        part = merged(moved[:, :, pl.ds(at, 2 * cols)])
        out_ref[:, pl.ds(at, 2 * cols)] = dot1(swap_ref[...], part).astype(BF16)


def call(kernel, out_shape, out_dtype, scratch, *args, name, flops):
    size = sum(a.size * a.dtype.itemsize for a in args)
    return pl.pallas_call(
        kernel,
        out_shape=jax.ShapeDtypeStruct(out_shape, out_dtype),
        in_specs=[VMEM] * len(args),
        out_specs=VMEM,
        scratch_shapes=scratch,
        compiler_params=pltpu.CompilerParams(vmem_limit_bytes=50 * 2**20),
        cost_estimate=pl.CostEstimate(flops=flops, bytes_accessed=size, transcendentals=0),
        name=name,
    )(*args)


def body(prior, diffusivity, site, quantities, weightings):
    m, rows, width = prior.shape
    patches = lax.axis_size("mem")
    cols = width // patches
    members = m * patches
    obs = site.shape[-1]

    def edge(two_rows, one_row):
        high, low = halves(one_row)
        return jnp.concatenate(
            [jnp.transpose(two_rows, (1, 0, 2)).reshape(2 * m, width), high, low], axis=0
        )

    low, high = exchange(
        edge(prior[:, :2], diffusivity[:1]), edge(prior[:, -2:], diffusivity[-1:]), "space"
    )

    def split(got):
        return (
            got[: 2 * m].reshape(2, m, width),
            got[2 * m : 2 * m + 1].astype(F32) + got[2 * m + 1 :].astype(F32),
        )

    (low_x, low_d), (high_x, high_d) = split(low), split(high)
    d_ext = jnp.concatenate([low_d, diffusivity, high_d], axis=0)[:, None, :]
    padded = width + 2 * PAD
    fresh = call(
        forecast_kernel,
        (patches, rows, m, cols),
        BF16,
        [pltpu.VMEM((rows + 4, m, padded), F32), pltpu.VMEM((rows + 4, m, padded), F32)],
        prior.reshape(m * rows, width),
        swap_matrix(rows, m),
        d_ext,
        low_x,
        high_x,
        name="forecast",
        flops=2 * (m * rows) ** 2 * width,
    )
    patch = lax.all_to_all(fresh, "mem", split_axis=0, concat_axis=0, tiled=True)
    own = call(
        observe_kernel,
        (members + 8, members),
        F32,
        [pltpu.VMEM((members, obs), F32)],
        patch,
        site[0],
        quantities[0],
        weightings[0],
        name="observe",
        flops=2 * members * obs * (rows * cols + members),
    )
    sent = own.astype(BF16)
    low, high = exchange(sent, sent, "mem")
    band = own + 0.5 * (low.astype(F32) + high.astype(F32))
    sent = band.astype(BF16)
    low, high = exchange(sent, sent, "space")
    gram = band + 0.5 * (low.astype(F32) + high.astype(F32))
    updated = call(
        analyse_kernel,
        (patches, rows, m, cols),
        BF16,
        [],
        gram,
        patch,
        name="analyse",
        flops=2 * members * members * (rows * cols + 90 * members),
    )
    back = lax.all_to_all(updated, "mem", split_axis=0, concat_axis=0, tiled=True)
    low, high = exchange(back[:, 0], back[:, -1], "space")
    out = call(
        finish_kernel,
        (m * rows, width),
        BF16,
        [pltpu.VMEM((rows + 2, m, padded), F32), pltpu.VMEM((rows, m, width), BF16)],
        back,
        swap_matrix(m, rows),
        diffusivity[:, None, :],
        low,
        high,
        name="finish",
        flops=2 * (m * rows) ** 2 * width,
    )
    return out.reshape(m, rows, width)


def solution(mesh):
    return jax.shard_map(
        body,
        mesh=mesh,
        in_specs=(
            P("mem", "space", None),
            P("space", None),
            P("space", "mem", None),
            P("space", "mem", None),
            P("space", "mem", None),
        ),
        out_specs=P("mem", "space", None),
        check_vma=False,
    )
```

time: 288 us -> 189 us (0.66)
  local copies, waits for them, and re-layouts: 85.6 us -> 4.11 us
  blocking collectives: 58.3 us -> 109 us
  waiting for transfers between devices: 67.8 us -> 20.7 us
  Pallas kernels: 0 us -> 34.1 us
  starting transfers between devices: 43.9 us -> 18.8 us
  matrix products: 15.8 us -> 0 us
  other arithmetic: 12.9 us -> 1.68 us
    all_to_all x1 -> x2, blocking collectives: 58.3 us -> 109 us  [the longest x1 54.8 us: body(): lax.all_to_all(updated, 'mem', split_axis=0, concat_axis=0, tiled=True)]
    all_to_all x1 -> x0, waiting for transfers between devices: 40.9 us -> none  [body(): lax.all_to_all(advanced_sample, 'mem', split_axis=2, concat_axis=0, tiled...]
    unnamed x16 -> x10, local copies, waits for them, and re-layouts: 38.1 us -> 0.03 us
    pallas_call x0 -> x4, Pallas kernels: none -> 34.1 us  [call(): pl.pallas_call(kernel, out_shape=jax.ShapeDtypeStruct(out_shape, out_dtyp...]
    all_to_all x3 -> x0, local copies, waits for them, and re-layouts: 22.3 us -> none  [the longest x1 16.9 us: body(): lax.all_to_all(advanced_sample, 'mem', split_axis=2, concat_axis=0, tiled...]
    ppermute x14 -> x8, starting transfers between devices: 37.3 us -> 18.8 us  [the longest x4 13.6 us: exchange(): lax.ppermute(high_edge, axis, forward)]
    convert_element_type x3 -> x0, local copies, waits for them, and re-layouts: 16.8 us -> none  [the longest x1 14.3 us: body(): advanced_sample = present_sample.astype(jnp.bfloat16)]
    dot_general x35 -> x0, matrix products: 15.8 us -> none  [the longest x10 5.96 us: newton(): jnp.dot(root_part, factor, precision=HIGHEST)]
  transfers between devices with their start and end apart: 15 -> 8, of which waited for: 10 -> 7; matrix products, arithmetic and copies ran while one was open for 0% -> 0% of each run, Pallas kernels for 0% -> 0%
where the time goes in v1:
time: 189 us; the launch traced here: 188 us
  blocking collectives  109 us (58%)
  Pallas kernels  34.1 us (18%)
  waiting for transfers between devices  20.7 us (11%)
  starting transfers between devices  18.8 us (10%)
  local copies, waits for them, and re-layouts  4.11 us (2%)
    all_to_all x1, blocking collectives, body(): lax.all_to_all(updated, 'mem', split_axis=0, concat_axis=0, tiled=True)  54.8 us
    all_to_all x1, blocking collectives, body(): lax.all_to_all(fresh, 'mem', split_axis=0, concat_axis=0, tiled=True)  53.8 us
    pallas_call x4, Pallas kernels, call(): pl.pallas_call(kernel, out_shape=jax.ShapeDtypeStruct(out_shape, out_dtyp...  34.1 us
    ppermute x4, waiting for transfers between devices, exchange(): lax.ppermute(low_edge, axis, backward)  16 us
    ppermute x4, starting transfers between devices, exchange(): lax.ppermute(high_edge, axis, forward)  13.6 us
    ppermute x4, starting transfers between devices, exchange(): lax.ppermute(low_edge, axis, backward)  5.17 us
    ppermute x4, waiting for transfers between devices, exchange(): lax.ppermute(high_edge, axis, forward)  4.75 us
  transfers between devices with their start and end apart: 8, of which 7 were waited for; matrix products, arithmetic and copies ran while one was open for 0% of the time, Pallas kernels for 0%

profile of v1, /device:TPU:0, one launch (start us, length us, event | category | flops | bytes accessed | tf_op | source)
XLA Modules:
  0.0 188.3 jit_solution(5346798770921981180)
XLA Ops:
  0.0 1.0 fusion.6
  1.0 1.0 subtract_convert_fusion.1
  2.0 2.1 %slice_bitcast_fusion.1 = (bf16[2,16,4096]{2,0,1:T(2,128)(2,1)S(1)}, bf16[2,16,4096]{2,0,1:T(2,128)(2,1)S(1)}) fusion(bf16[16,16,4096]{2,1,0:T(8,128)(2,1)} %param.5), kind=kLoop, calls=%fused_computation.6 | loop fusion | bytes 1048576 | tf_op jit(solution)/shard_map/transpose | solution.py:199
  4.2 0.2 copy.11
  4.4 1.3 collective-permute-start.1
  5.7 0.2 copy.10
  5.9 4.9 %collective-permute-start = (bf16[34,4096]{1,0:T(8,128)(2,1)S(1)}, bf16[34,4096]{1,0:T(8,128)(2,1)S(1)}, u32[]{:S(2)}, u32[]{:S(2)}) collective-permute-start(bf16[34,4096]{1,0:T(8,128)(2,1)S(1)} %pad_maximum_fusion.1), channel_id=1, source_target_pairs={{0,1},{2,3},{4,5},{6,7},{8,9},{10,11},{12,13},{14,15},{16,17},{18,... | collective-permute-start | bytes 835592 | tf_op jit(solution)/shard_map/ppermute | solution.py:22
  10.9 0.3 fusion.swap_ref
  11.2 5.2 %collective-permute-done.1 = bf16[34,4096]{1,0:T(8,128)(2,1)S(1)} collective-permute-done((bf16[34,4096]{1,0:T(8,128)(2,1)S(1)}, bf16[34,4096]{1,0:T(8,128)(2,1)S(1)}, u32[]{:S(2)}, u32[]{:S(2)}) %collective-permute-start.1) | collective-permute-done | bytes 278560 | tf_op jit(solution)/shard_map/ppermute | solution.py:22
  16.4 1.4 collective-permute-done
  17.8 0.1 pad_maximum_fusion
  17.9 0.3 broadcast_in_dim.6.d_ref
  18.3 10.8 %forecast.1 = bf16[16,16,16,256]{3,2,1,0:T(8,128)(2,1)S(1)} custom-call(bf16[256,4096]{1,0:T(8,128)(2,1)} %bitcast.26, bf16[256,256]{1,0:T(8,128)(2,1)S(1)} %fusion.swap_ref, f32[18,1,4096]{2,1,0:T(1,128)S(1)} %broadcast_in_dim.6.d_ref, bf16[2,16,4096]{2,1,0:T(8,128)(2,1)S(1)} %bitcast.21, bf16[2,16,4096]{2,1,0:T(8,128)(2,1)S(1)} %bitcast.22), custom_call_target="tpu_custom_call" | custom-call | flops 536870912 | bytes 3047424 | tf_op jit(solution)/shard_map/forecast/pallas_call | solution.py:177
  29.1 53.8 %all_to_all.10.patch_ref = bf16[16,16,16,256]{3,2,1,0:T(8,128)(2,1)S(1)} all-to-all(bf16[16,16,16,256]{3,2,1,0:T(8,128)(2,1)S(1)} %forecast.1), channel_id=1, replica_groups=mesh['mem'=16,'space'=2] {'mem'}, dimensions={0} | all-to-all | bytes 4194304 | tf_op jit(solution)/shard_map/all_to_all | solution.py:228
  82.9 4.2 %observe.1 = f32[264,256]{1,0:T(8,128)S(1)} custom-call(bf16[16,16,16,256]{3,2,1,0:T(8,128)(2,1)S(1)} %all_to_all.10.patch_ref, s32[1,512]{1,0:T(1,128)S(1)} %bitcast.23, f32[1,512]{1,0:T(1,128)S(1)} %bitcast.24, f32[1,512]{1,0:T(1,128)S(1)} %bitcast.25), custom_call_target="tpu_custom_call" | custom-call | flops 1140850688 | bytes 2103296 | tf_op jit(solution)/shard_map/observe/pallas_call | solution.py:177
  87.1 2.9 %collective-permute-start.2 = (bf16[264,256]{1,0:T(8,128)(2,1)S(1)}, bf16[264,256]{1,0:T(8,128)(2,1)S(1)}, u32[]{:S(2)}, u32[]{:S(2)}) collective-permute-start(bf16[264,256]{1,0:T(8,128)(2,1)S(1)} %convert_element_type.65), channel_id=1, source_target_pairs={{0,2},{2,4},{4,6},{6,8},{8,10},{10,12},{12,14},{14,16},{16,18},{18... | collective-permute-start | bytes 405512 | tf_op jit(solution)/shard_map/ppermute | solution.py:22
  90.0 1.3 collective-permute-start.3
  91.3 1.9 %collective-permute-done.3 = bf16[264,256]{1,0:T(8,128)(2,1)S(1)} collective-permute-done((bf16[264,256]{1,0:T(8,128)(2,1)S(1)}, bf16[264,256]{1,0:T(8,128)(2,1)S(1)}, u32[]{:S(2)}, u32[]{:S(2)}) %collective-permute-start.3) | collective-permute-done | bytes 135200 | tf_op jit(solution)/shard_map/ppermute | solution.py:22
  93.3 0.1 fusion.1
  93.3 4.3 %collective-permute-start.4 = (bf16[264,256]{1,0:T(8,128)(2,1)S(1)}, bf16[264,256]{1,0:T(8,128)(2,1)S(1)}, u32[]{:S(2)}, u32[]{:S(2)}) collective-permute-start(bf16[264,256]{1,0:T(8,128)(2,1)S(1)} %fusion.1), channel_id=1, source_target_pairs={{0,1},{2,3},{4,5},{6,7},{8,9},{10,11},{12,13},{14,15},{16,17},{18,... | collective-permute-start | bytes 405512 | tf_op jit(solution)/shard_map/ppermute | solution.py:22
  97.7 1.3 collective-permute-start.5
  99.0 1.2 collective-permute-done.4
  100.2 4.4 %collective-permute-done.5 = bf16[264,256]{1,0:T(8,128)(2,1)S(1)} collective-permute-done((bf16[264,256]{1,0:T(8,128)(2,1)S(1)}, bf16[264,256]{1,0:T(8,128)(2,1)S(1)}, u32[]{:S(2)}, u32[]{:S(2)}) %collective-permute-start.5) | collective-permute-done | bytes 135200 | tf_op jit(solution)/shard_map/ppermute | solution.py:22
  104.6 0.1 multiply_add_fusion.gram_ref
  104.7 12.2 %analyse.1 = bf16[16,16,16,256]{3,2,1,0:T(8,128)(2,1)S(1)} custom-call(f32[264,256]{1,0:T(8,128)S(1)} %multiply_add_fusion.gram_ref, bf16[16,16,16,256]{3,2,1,0:T(8,128)(2,1)} %copy-done), custom_call_target="tpu_custom_call" | custom-call | flops 3556769792 | bytes 2367488 | tf_op jit(solution)/shard_map/analyse/pallas_call | solution.py:177
  116.9 54.8 %all_to_all.11.x_ref = bf16[16,16,16,256]{3,2,1,0:T(8,128)(2,1)S(1)} all-to-all(bf16[16,16,16,256]{3,2,1,0:T(8,128)(2,1)S(1)} %analyse.1), channel_id=1, replica_groups=mesh['mem'=16,'space'=2] {'mem'}, dimensions={0} | all-to-all | bytes 4194304 | tf_op jit(solution)/shard_map/all_to_all | solution.py:257
  171.8 1.4 collective-permute-start.6
  173.2 1.3 collective-permute-start.7
  174.5 0.3 broadcast_in_dim.7.d_ref
  174.7 2.1 %collective-permute-done.6.low_ref = bf16[16,16,256]{2,1,0:T(8,128)(2,1)S(1)} collective-permute-done((bf16[16,16,256]{2,1,0:T(8,128)(2,1)S(1)}, bf16[16,16,256]{2,1,0:T(8,128)(2,1)S(1)}, u32[]{:S(2)}, u32[]{:S(2)}) %collective-permute-start.6) | collective-permute-done | bytes 131104 | tf_op jit(solution)/shard_map/ppermute | solution.py:22
  176.9 4.4 %collective-permute-done.7.high_ref = bf16[16,16,256]{2,1,0:T(8,128)(2,1)S(1)} collective-permute-done((bf16[16,16,256]{2,1,0:T(8,128)(2,1)S(1)}, bf16[16,16,256]{2,1,0:T(8,128)(2,1)S(1)}, u32[]{:S(2)}, u32[]{:S(2)}) %collective-permute-start.7) | collective-permute-done | bytes 131104 | tf_op jit(solution)/shard_map/ppermute | solution.py:22
  181.3 6.9 %finish.1 = bf16[256,4096]{1,0:T(8,128)(2,1)} custom-call(bf16[16,16,16,256]{3,2,1,0:T(8,128)(2,1)S(1)} %all_to_all.11.x_ref, bf16[256,256]{1,0:T(8,128)(2,1)S(1)} %fusion.swap_ref, f32[16,1,4096]{2,1,0:T(1,128)S(1)} %broadcast_in_dim.7.d_ref, bf16[16,16,256]{2,1,0:T(8,128)(2,1)S(1)} %collective-permute-done.6.low_ref, ...), custom_call_target="tpu_custom_call" | custom-call | flops 536870912 | bytes 2752512 | tf_op jit(solution)/shard_map/finish/pallas_call | solution.py:177
  (22 shorter events, 0.3 us)
Async XLA Ops:
  0.0 17.8 %copy-start.4 = (f32[16,4096]{1,0:T(8,128)S(1)}, f32[16,4096]{1,0:T(8,128)}, u32[]{:S(2)}) copy-start(f32[16,4096]{1,0:T(8,128)} %param.6) | copy-start | bytes 786436
  4.4 12.0 %collective-permute-start.1 = (bf16[34,4096]{1,0:T(8,128)(2,1)S(1)}, bf16[34,4096]{1,0:T(8,128)(2,1)S(1)}, u32[]{:S(2)}, u32[]{:S(2)}) collective-permute-start(bf16[34,4096]{1,0:T(8,128)(2,1)S(1)} %pad_maximum_fusion.2), channel_id=1, source_target_pairs={{1,0},{3,2},{5,4},{7,6},{9,8},{11,10},{13,12},{15,14},{17,16},{19,... | collective-permute-start | bytes 835592 | tf_op jit(solution)/shard_map/ppermute | solution.py:22
  5.9 11.9 %collective-permute-start = (bf16[34,4096]{1,0:T(8,128)(2,1)S(1)}, bf16[34,4096]{1,0:T(8,128)(2,1)S(1)}, u32[]{:S(2)}, u32[]{:S(2)}) collective-permute-start(bf16[34,4096]{1,0:T(8,128)(2,1)S(1)} %pad_maximum_fusion.1), channel_id=1, source_target_pairs={{0,1},{2,3},{4,5},{6,7},{8,9},{10,11},{12,13},{14,15},{16,17},{18,... | collective-permute-start | bytes 835592 | tf_op jit(solution)/shard_map/ppermute | solution.py:22
  29.1 53.9 %copy-start.1 = (s32[1,1,512]{2,1,0:T(1,128)S(1)}, s32[1,1,512]{2,1,0:T(1,128)}, u32[]{:S(2)}) copy-start(s32[1,1,512]{2,1,0:T(1,128)} %param.7) | copy-start | bytes 6148
  29.1 53.8 %copy-start.2 = (f32[1,1,512]{2,1,0:T(1,128)S(1)}, f32[1,1,512]{2,1,0:T(1,128)}, u32[]{:S(2)}) copy-start(f32[1,1,512]{2,1,0:T(1,128)} %param.8) | copy-start | bytes 6148
  29.1 53.8 %copy-start.3 = (f32[1,1,512]{2,1,0:T(1,128)S(1)}, f32[1,1,512]{2,1,0:T(1,128)}, u32[]{:S(2)}) copy-start(f32[1,1,512]{2,1,0:T(1,128)} %param.9) | copy-start | bytes 6148
  82.9 4.2 %copy-start = (bf16[16,16,16,256]{3,2,1,0:T(8,128)(2,1)}, bf16[16,16,16,256]{3,2,1,0:T(8,128)(2,1)S(1)}, u32[]{:S(2)}) copy-start(bf16[16,16,16,256]{3,2,1,0:T(8,128)(2,1)S(1)} %all_to_all.10.patch_ref) | copy-start | bytes 6291460
  87.1 4.2 %collective-permute-start.2 = (bf16[264,256]{1,0:T(8,128)(2,1)S(1)}, bf16[264,256]{1,0:T(8,128)(2,1)S(1)}, u32[]{:S(2)}, u32[]{:S(2)}) collective-permute-start(bf16[264,256]{1,0:T(8,128)(2,1)S(1)} %convert_element_type.65), channel_id=1, source_target_pairs={{0,2},{2,4},{4,6},{6,8},{8,10},{10,12},{12,14},{14,16},{16,18},{18... | collective-permute-start | bytes 405512 | tf_op jit(solution)/shard_map/ppermute | solution.py:22
  90.0 3.2 %collective-permute-start.3 = (bf16[264,256]{1,0:T(8,128)(2,1)S(1)}, bf16[264,256]{1,0:T(8,128)(2,1)S(1)}, u32[]{:S(2)}, u32[]{:S(2)}) collective-permute-start(bf16[264,256]{1,0:T(8,128)(2,1)S(1)} %convert_element_type.65), channel_id=1, source_target_pairs={{2,0},{4,2},{6,4},{8,6},{10,8},{12,10},{14,12},{16,14},{18,16},{20... | collective-permute-start | bytes 405512 | tf_op jit(solution)/shard_map/ppermute | solution.py:22
  93.3 6.9 %collective-permute-start.4 = (bf16[264,256]{1,0:T(8,128)(2,1)S(1)}, bf16[264,256]{1,0:T(8,128)(2,1)S(1)}, u32[]{:S(2)}, u32[]{:S(2)}) collective-permute-start(bf16[264,256]{1,0:T(8,128)(2,1)S(1)} %fusion.1), channel_id=1, source_target_pairs={{0,1},{2,3},{4,5},{6,7},{8,9},{10,11},{12,13},{14,15},{16,17},{18,... | collective-permute-start | bytes 405512 | tf_op jit(solution)/shard_map/ppermute | solution.py:22
  97.7 6.9 %collective-permute-start.5 = (bf16[264,256]{1,0:T(8,128)(2,1)S(1)}, bf16[264,256]{1,0:T(8,128)(2,1)S(1)}, u32[]{:S(2)}, u32[]{:S(2)}) collective-permute-start(bf16[264,256]{1,0:T(8,128)(2,1)S(1)} %fusion.1), channel_id=1, source_target_pairs={{1,0},{3,2},{5,4},{7,6},{9,8},{11,10},{13,12},{15,14},{17,16},{19,... | collective-permute-start | bytes 405512 | tf_op jit(solution)/shard_map/ppermute | solution.py:22
  171.8 5.1 %collective-permute-start.6 = (bf16[16,16,256]{2,1,0:T(8,128)(2,1)S(1)}, bf16[16,16,256]{2,1,0:T(8,128)(2,1)S(1)}, u32[]{:S(2)}, u32[]{:S(2)}) collective-permute-start(bf16[16,16,256]{2,1,0:T(8,128)(2,1)S(1)} %get-tuple-element.6), channel_id=1, source_target_pairs={{0,1},{2,3},{4,5},{6,7},{8,9},{10,11},{12,13},{14,15},{16,17},{18,... | collective-permute-start | bytes 393224 | tf_op jit(solution)/shard_map/ppermute | solution.py:22
  173.2 8.1 %collective-permute-start.7 = (bf16[16,16,256]{2,1,0:T(8,128)(2,1)S(1)}, bf16[16,16,256]{2,1,0:T(8,128)(2,1)S(1)}, u32[]{:S(2)}, u32[]{:S(2)}) collective-permute-start(bf16[16,16,256]{2,1,0:T(8,128)(2,1)S(1)} %get-tuple-element.5), channel_id=1, source_target_pairs={{1,0},{3,2},{5,4},{7,6},{9,8},{11,10},{13,12},{15,14},{17,16},{19,... | collective-permute-start | bytes 393224 | tf_op jit(solution)/shard_map/ppermute | solution.py:22

commit v2 on v1

v2 whole, which is shorter than its diff:
```python
import functools
import math

import jax
import jax.numpy as jnp
from jax import lax
from jax.experimental import pallas as pl
from jax.experimental.pallas import tpu as pltpu
from jax.sharding import PartitionSpec as P

ITERS = 10
PAD = 128
F32 = jnp.float32
BF16 = jnp.bfloat16
MESH = pl.DeviceIdType.MESH
VMEM = pl.BlockSpec(memory_space=pltpu.VMEM)


def exchange(low_edge, high_edge, axis):
    count = lax.axis_size(axis)
    forward = [(i, i + 1) for i in range(count - 1)]
    backward = [(target, source) for source, target in forward]
    return lax.ppermute(high_edge, axis, forward), lax.ppermute(low_edge, axis, backward)


def swap_matrix(outer, inner):
    size = outer * inner
    row = lax.broadcasted_iota(jnp.int32, (size, size), 0)
    col = lax.broadcasted_iota(jnp.int32, (size, size), 1)
    return ((row % inner) * outer + row // inner == col).astype(BF16)


def merged(block):
    a, m, c = block.shape
    if m % 16 == 0:
        return block.reshape(a * m, c)
    return block.astype(F32).reshape(a * m, c).astype(BF16)


def halves(value):
    high = value.astype(BF16)
    return high, (value - high.astype(F32)).astype(BF16)


def dot1(a, b):
    return jnp.dot(a, b, preferred_element_type=F32)


def dot3(a, b):
    ah, al = a
    bh, bl = b
    return dot1(ah, bh) + (dot1(ah, bl) + dot1(al, bh))


def step(src, row, diffusion, at, cols):
    lo = PAD + at
    mid = src[row, :, lo : lo + cols]
    around = (
        src[row - 1, :, lo : lo + cols]
        + src[row + 1, :, lo : lo + cols]
        + src[row, :, lo - 1 : lo - 1 + cols]
        + src[row, :, lo + 1 : lo + 1 + cols]
    )
    return mid + diffusion * (around - 4.0 * mid)


def clear_pads(buf, width):
    rows, m, _ = buf.shape
    buf[:, :, :PAD] = jnp.zeros((rows, m, PAD), F32)
    buf[:, :, PAD + width :] = jnp.zeros((rows, m, PAD), F32)


class Peers:
    def __init__(self, n, spaces):
        self.n = n
        self.me = lax.axis_index("mem")
        self.space = lax.axis_index("space")
        self.has_low = self.space > 0
        self.has_high = self.space < spaces - 1
        self.order = []
        for k in reversed(range(1, n)):
            peer, bit = self.me, 1
            while bit < n:
                if k & bit:
                    peer = peer + bit * (1 - 2 * ((self.me // bit) % 2))
                bit *= 2
            self.order.append(peer)

    def sides(self):
        return ((self.has_low, self.space - 1), (self.has_high, self.space + 1))

    def greet(self):
        barrier = pltpu.get_barrier_semaphore()
        for peer in self.order:
            pl.semaphore_signal(barrier, inc=1, device_id={"mem": peer}, device_id_type=MESH)
        for has, other in self.sides():

            @pl.when(has)
            def _():
                pl.semaphore_signal(barrier, inc=1, device_id={"space": other}, device_id_type=MESH)

    def meet(self):
        barrier = pltpu.get_barrier_semaphore()
        beside = self.has_low.astype(jnp.int32) + self.has_high.astype(jnp.int32)
        pl.semaphore_wait(barrier, self.n - 1 + beside)


class Blocks:
    def __init__(self, peers, src, dst, groups, send, recv):
        self.peers, self.src, self.dst = peers, src, dst
        self.groups, self.sems = groups, (send, recv)

    def copy(self, g, i, slot):
        first, last = self.groups[g]
        peer = self.peers.order[i]
        send, recv = self.sems
        return pltpu.make_async_remote_copy(
            src_ref=self.src.at[peer, first:last],
            dst_ref=self.dst.at[slot, first:last],
            send_sem=send.at[g, i],
            recv_sem=recv.at[g, i],
            device_id={"mem": peer},
            device_id_type=MESH,
        )

    def start(self, g):
        for i in range(len(self.peers.order)):
            self.copy(g, i, self.peers.me).start()
        first, last = self.groups[g]
        me = self.peers.me
        self.dst[me, first:last] = self.src[me, first:last]

    def arrive(self, g):
        for i in range(len(self.peers.order)):
            self.copy(g, i, self.peers.order[i]).wait_recv()

    def finish(self):
        for g in range(len(self.groups)):
            for i in range(len(self.peers.order)):
                self.copy(g, i, self.peers.me).wait_send()


def beside(src, dst, sems, slot, other):
    send, recv = sems
    return pltpu.make_async_remote_copy(
        src_ref=src,
        dst_ref=dst,
        send_sem=send.at[slot],
        recv_sem=recv.at[slot],
        device_id={"space": other},
        device_id_type=MESH,
    )


def cut(first, last, parts):
    size = -(-(last - first) // parts)
    return [(a, min(a + size, last)) for a in range(first, last, size)]


def forecast_groups(rows):
    return cut(2, rows - 2, 3) + [(0, 2), (rows - 2, rows)]


def forecast_kernel(
    spaces, x_ref, swap_ref, d_ref, site_ref, value_ref, weight_ref, patch_ref, gram_ref,
    xs, v1, fresh, edge_out, edge_in, d_in, acc, send, recv, side_send, side_recv,
):
    patches, rows, m, cols = patch_ref.shape
    width = patches * cols
    members = patches * m
    obs = site_ref.shape[1]
    peers = Peers(patches, spaces)
    peers.greet()
    groups = forecast_groups(rows)
    blocks = Blocks(peers, fresh, patch_ref, groups, send, recv)
    clear_pads(xs, width)
    clear_pads(v1, width)

    for c in range(patches // 2):
        at = c * 2 * cols
        part = dot1(swap_ref[...], x_ref[:, at : at + 2 * cols]).reshape(rows, m, 2 * cols)
        xs[2 : rows + 2, :, PAD + at : PAD + at + 2 * cols] = part
        edge_out[0, :, :, at : at + 2 * cols] = part[:2].astype(BF16)
        edge_out[1, :, :, at : at + 2 * cols] = part[rows - 2 :].astype(BF16)

    peers.meet()
    side = (side_send, side_recv)

    def halo(k, other):
        return (
            beside(edge_out.at[k], edge_in.at[1 - k], side, k, other),
            beside(d_ref.at[0 if k == 0 else rows - 1], d_in.at[1 - k], side, 2 + k, other),
        )

    def halo_in(k, other):
        return (
            beside(edge_out.at[k], edge_in.at[k], side, 1 - k, other),
            beside(d_ref.at[0], d_in.at[k], side, 3 - k, other),
        )

    for k, (has, other) in enumerate(peers.sides()):

        @pl.when(has)
        def _():
            for copy in halo(k, other):
                copy.start()

    def first_step(r, d_row):
        for q in range(patches):
            at = q * cols
            v1[r, :, PAD + at : PAD + at + cols] = step(xs, r, d_row(at), at, cols)

    def second_step(r):
        for q in range(patches):
            at = q * cols
            fresh[q, r - 2] = step(v1, r, d_ref[r - 2, :, at : at + cols], at, cols).astype(BF16)

    done = 3
    for g in range(len(groups) - 2):
        first, last = groups[g]

        @pl.loop(done, last + 3)
        def _(r):
            first_step(r, lambda at: d_ref[r - 2, :, at : at + cols])

        done = last + 3

        @pl.loop(first + 2, last + 2)
        def _(r):
            second_step(r)

        blocks.start(g)

    for k, (has, other) in enumerate(peers.sides()):
        row = 0 if k == 0 else rows + 2

        @pl.when(has)
        def _():
            for copy in halo_in(k, other):
                copy.wait_recv()
            xs[row : row + 2, :, PAD : PAD + width] = edge_in[k].astype(F32)

        @pl.when(jnp.logical_not(has))
        def _():
            xs[row : row + 2, :, PAD : PAD + width] = jnp.zeros((2, m, width), F32)
            d_in[k] = jnp.zeros((1, width), F32)

    for k in range(2):
        outer, inner = (1, 2) if k == 0 else (rows + 2, rows + 1)
        first_step(outer, lambda at: d_in[k, :, at : at + cols])
        first_step(inner, lambda at: d_ref[inner - 2, :, at : at + cols])
        g = len(groups) - 2 + k

        @pl.loop(groups[g][0] + 2, groups[g][1] + 2)
        def _(r):
            second_step(r)

        blocks.start(g)

    acc[...] = jnp.zeros_like(acc)
    for g, (first, last) in enumerate(groups):
        blocks.arrive(g)

        @pl.loop(first, last)
        def _(r):
            cell = lax.broadcasted_iota(jnp.int32, (cols, obs), 0) + r * cols
            picked = jnp.where(cell == site_ref[...], 1.0, 0.0).astype(BF16)
            acc[...] += dot1(merged(patch_ref[:, r]), picked)

    observed = acc[...]
    obs_mean = jnp.sum(observed, axis=0, keepdims=True) * (1.0 / members)
    root = jnp.sqrt(weight_ref[...])
    spread = ((observed - obs_mean) * root).astype(BF16)
    innovation = ((value_ref[...] - obs_mean) * root).astype(BF16)
    contract = (((1,), (1,)), ((), ()))
    gram_ref[0:members, :] = lax.dot_general(spread, spread, contract, preferred_element_type=F32)
    wide = jnp.broadcast_to(innovation.astype(F32), (8, obs)).astype(BF16)
    gram_ref[members : members + 8, :] = lax.dot_general(
        wide, spread, contract, preferred_element_type=F32
    )
    blocks.finish()
    for k, (has, other) in enumerate(peers.sides()):

        @pl.when(has)
        def _():
            for copy in halo(k, other):
                copy.wait_send()


def transform_of(gram, vector, members):
    identity = (
        lax.broadcasted_iota(jnp.int32, (members, members), 0)
        == lax.broadcasted_iota(jnp.int32, (members, members), 1)
    ).astype(F32)
    system = gram + (members - 1.0) * identity
    frob = jnp.sqrt(jnp.sum(jnp.sum(system * system, axis=1, keepdims=True), axis=0, keepdims=True))
    root_part = system / frob
    factor = 1.5 * identity - 0.5 * root_part
    root_part = dot3(halves(root_part), halves(factor))
    inverse_part = factor
    for index in range(1, ITERS):
        r, z = halves(root_part), halves(inverse_part)
        f = halves(1.5 * identity - 0.5 * dot3(z, r))
        if index < ITERS - 1:
            root_part = dot3(r, f)
        inverse_part = dot3(f, z)
    inverse_root = inverse_part / jnp.sqrt(frob)
    z = halves(inverse_root)
    weights = dot3(halves(dot3(halves(vector), z)), z)[0:1, :]
    return (math.sqrt(members - 1.0) * inverse_root + weights).astype(BF16)


def analyse_groups(rows):
    return [(0, 1), (rows - 1, rows)] + cut(1, rows - 1, 3)


def analyse_kernel(
    spaces, gram_ref, patch_ref, swap_ref, d_ref, out_ref,
    updated, back, edge_in, turned, xs, moved, send, recv, side_send, side_recv,
):
    patches, rows, m, cols = patch_ref.shape
    width = patches * cols
    members = patches * m
    peers = Peers(patches, spaces)
    peers.greet()
    groups = analyse_groups(rows)
    blocks = Blocks(peers, updated, back, groups, send, recv)
    clear_pads(xs, width)
    turned[...] = transform_of(gram_ref[0:members, :], gram_ref[members:, :], members)
    peers.meet()

    for g, (first, last) in enumerate(groups):

        @pl.loop(first, last)
        def _(r):
            cells = merged(patch_ref[:, r]).astype(F32)
            mean = jnp.sum(cells, axis=0, keepdims=True) * (1.0 / members)
            result = mean + dot1(turned[...], (cells - mean).astype(BF16))
            updated[:, r] = result.reshape(patches, m, cols).astype(BF16)

        blocks.start(g)

    side = (side_send, side_recv)

    def halo(k, other):
        return beside(back.at[:, 0 if k == 0 else rows - 1], edge_in.at[1 - k], side, k, other)

    def halo_in(k, other):
        return beside(back.at[:, 0], edge_in.at[k], side, 1 - k, other)

    def take(r):
        for q in range(patches):
            xs[r + 1, :, PAD + q * cols : PAD + (q + 1) * cols] = back[q, r].astype(F32)

    def last_step(r):
        for q in range(patches):
            at = q * cols
            moved[r, :, at : at + cols] = step(
                xs, r + 1, d_ref[r, :, at : at + cols], at, cols
            ).astype(BF16)

    for k, (has, other) in enumerate(peers.sides()):
        blocks.arrive(k)
        take(0 if k == 0 else rows - 1)

        @pl.when(has)
        def _():
            halo(k, other).start()

    done = 1
    for g in range(2, len(groups)):
        first, last = groups[g]
        blocks.arrive(g)

        @pl.loop(first, last)
        def _(r):
            take(r)

        upto = last if g == len(groups) - 1 else last - 1

        @pl.loop(done, upto)
        def _(r):
            last_step(r)

        done = upto
        if g == 2:
            for k, (has, other) in enumerate(peers.sides()):
                row = 0 if k == 0 else rows + 1

                @pl.when(has)
                def _():
                    halo_in(k, other).wait_recv()
                    for q in range(patches):
                        xs[row, :, PAD + q * cols : PAD + (q + 1) * cols] = edge_in[k, q].astype(F32)

                @pl.when(jnp.logical_not(has))
                def _():
                    xs[row, :, PAD : PAD + width] = jnp.zeros((m, width), F32)

            last_step(0)
    last_step(rows - 1)

    for c in range(patches // 2):
        at = c * 2 * cols
        part = merged(moved[:, :, at : at + 2 * cols])
        out_ref[:, at : at + 2 * cols] = dot1(swap_ref[...], part).astype(BF16)
    blocks.finish()
    for k, (has, other) in enumerate(peers.sides()):

        @pl.when(has)
        def _():
            halo(k, other).wait_send()


def call(kernel, shapes, scratch, *args, name, number, flops):
    size = sum(a.size * a.dtype.itemsize for a in args)
    return pl.pallas_call(
        kernel,
        out_shape=shapes,
        in_specs=[VMEM] * len(args),
        out_specs=jax.tree.map(lambda _: VMEM, shapes),
        scratch_shapes=scratch,
        compiler_params=pltpu.CompilerParams(
            vmem_limit_bytes=50 * 2**20, collective_id=number, has_side_effects=True
        ),
        cost_estimate=pl.CostEstimate(flops=flops, bytes_accessed=size, transcendentals=0),
        name=name,
    )(*args)


def body(prior, diffusivity, site, quantities, weightings):
    m, rows, width = prior.shape
    patches = lax.axis_size("mem")
    spaces = lax.axis_size("space")
    cols = width // patches
    members = m * patches
    obs = site.shape[-1]
    padded = width + 2 * PAD
    d3 = diffusivity[:, None, :]
    dma = pltpu.SemaphoreType.DMA
    many = len(forecast_groups(rows))
    patch, own = call(
        functools.partial(forecast_kernel, spaces),
        (
            jax.ShapeDtypeStruct((patches, rows, m, cols), BF16),
            jax.ShapeDtypeStruct((members + 8, members), F32),
        ),
        [
            pltpu.VMEM((rows + 4, m, padded), F32),
            pltpu.VMEM((rows + 4, m, padded), F32),
            pltpu.VMEM((patches, rows, m, cols), BF16),
            pltpu.VMEM((2, 2, m, width), BF16),
            pltpu.VMEM((2, 2, m, width), BF16),
            pltpu.VMEM((2, 1, width), F32),
            pltpu.VMEM((members, obs), F32),
            dma((many, patches - 1)),
            dma((many, patches - 1)),
            dma((4,)),
            dma((4,)),
        ],
        prior.reshape(m * rows, width),
        swap_matrix(rows, m),
        d3,
        site[0],
        quantities[0],
        weightings[0],
        name="forecast",
        number=0,
        flops=2 * (m * rows) ** 2 * width,
    )
    sent = own.astype(BF16)
    low, high = exchange(sent, sent, "mem")
    band = own + 0.5 * (low.astype(F32) + high.astype(F32))
    sent = band.astype(BF16)
    low, high = exchange(sent, sent, "space")
    gram = band + 0.5 * (low.astype(F32) + high.astype(F32))
    many = len(analyse_groups(rows))
    out = call(
        functools.partial(analyse_kernel, spaces),
        jax.ShapeDtypeStruct((m * rows, width), BF16),
        [
            pltpu.VMEM((patches, rows, m, cols), BF16),
            pltpu.VMEM((patches, rows, m, cols), BF16),
            pltpu.VMEM((2, patches, m, cols), BF16),
            pltpu.VMEM((members, members), BF16),
            pltpu.VMEM((rows + 2, m, padded), F32),
            pltpu.VMEM((rows, m, width), BF16),
            dma((many, patches - 1)),
            dma((many, patches - 1)),
            dma((2,)),
            dma((2,)),
        ],
        gram,
        patch,
        swap_matrix(m, rows),
        d3,
        name="analyse",
        number=1,
        flops=2 * members * members * (rows * cols + 90 * members),
    )
    return out.reshape(m, rows, width)


def solution(mesh):
    return jax.shard_map(
        body,
        mesh=mesh,
        in_specs=(
            P("mem", "space", None),
            P("space", None),
            P("space", "mem", None),
            P("space", "mem", None),
            P("space", "mem", None),
        ),
        out_specs=P("mem", "space", None),
        check_vma=False,
    )
```

time: 189 us -> 140 us (0.74)
  blocking collectives: 109 us -> 0 us
  Pallas kernels: 34.1 us -> 119 us
  waiting for transfers between devices: 20.7 us -> 3.92 us
  starting transfers between devices: 18.8 us -> 10.2 us
    all_to_all x2 -> x0, blocking collectives: 109 us -> none  [the longest x1 54.8 us: body(): lax.all_to_all(updated, 'mem', split_axis=0, concat_axis=0, tiled=True)]
    pallas_call x4 -> x2, Pallas kernels: 34.1 us -> 119 us  [call(): pl.pallas_call(kernel, out_shape=shapes, in_specs=[VMEM] * len(args), out...]
    ppermute x4 -> x2, waiting for transfers between devices: 16 us -> 1.22 us  [exchange(): lax.ppermute(low_edge, axis, backward)]
    ppermute x4 -> x2, starting transfers between devices: 13.6 us -> 7.6 us  [exchange(): lax.ppermute(high_edge, axis, forward)]
    unnamed x10 -> x9, local copies, waits for them, and re-layouts: 0.03 us -> 4.67 us
    ppermute x4 -> x2, starting transfers between devices: 5.17 us -> 2.58 us  [exchange(): lax.ppermute(low_edge, axis, backward)]
    transpose x3 -> x0, local copies, waits for them, and re-layouts: 2.42 us -> none  [edge(): jnp.transpose(two_rows, (1, 0, 2)).reshape(2 * m, width)]
    ppermute x4 -> x2, waiting for transfers between devices: 4.75 us -> 2.7 us  [exchange(): lax.ppermute(high_edge, axis, forward)]
  transfers between devices with their start and end apart: 8 -> 4, of which waited for: 7 -> 3; matrix products, arithmetic and copies ran while one was open for 0% -> 0% of each run, Pallas kernels for 0% -> 0%
where the time goes in v2:
time: 140 us; the launch traced here: 139 us
  Pallas kernels  119 us (85%)
  starting transfers between devices  10.2 us (7%)
  local copies, waits for them, and re-layouts  5.89 us (4%)
  waiting for transfers between devices  3.92 us (3%)
    pallas_call x2, Pallas kernels, call(): pl.pallas_call(kernel, out_shape=shapes, in_specs=[VMEM] * len(args), out...  119 us
    ppermute x2, starting transfers between devices, exchange(): lax.ppermute(high_edge, axis, forward)  7.6 us
    unnamed x9, local copies, waits for them, and re-layouts  4.67 us
  transfers between devices with their start and end apart: 4, of which 3 were waited for; matrix products, arithmetic and copies ran while one was open for 0% of the time, Pallas kernels for 0%

profile of v2, /device:TPU:0, one launch (start us, length us, event | category | flops | bytes accessed | tf_op | source)
XLA Modules:
  0.0 139.3 jit_solution(16464023425835059957)
XLA Ops:
  0.0 1.2 broadcast_in_dim.3.d_ref
  1.2 0.3 fusion.swap_ref
  1.5 0.0 copy-start
  1.5 0.7 copy-done
  2.2 0.0 copy-start.1
  2.2 0.7 copy-done.1
  2.9 0.0 copy-start.2
  2.9 0.7 copy-done.2
  3.6 59.3 %forecast.1 = (bf16[16,16,16,256]{3,2,1,0:T(8,128)(2,1)S(1)}, f32[264,256]{1,0:T(8,128)S(1)}) custom-call(bf16[256,4096]{1,0:T(8,128)(2,1)} %bitcast.9, bf16[256,256]{1,0:T(8,128)(2,1)S(1)} %fusion.swap_ref, f32[16,1,4096]{2,1,0:T(1,128)S(1)} %broadcast_in_dim.3.d_ref, s32[1,512]{1,0:T(1,128)S(1)} %bitcast.6, f32[1,512]{1,0:T(1,128)S(1)} %bitcast.7, ...), custom_call_target="tpu_custom_call" | custom-call | flops 536870912 | bytes 2496512 | tf_op jit(solution)/shard_map/forecast/pallas_call | solution.py:417
  62.9 0.0 copy-start.3
  62.9 1.3 copy-done.3
  64.2 1.3 collective-permute-start.1
  65.5 3.0 %collective-permute-start = (bf16[264,256]{1,0:T(8,128)(2,1)S(1)}, bf16[264,256]{1,0:T(8,128)(2,1)S(1)}, u32[]{:S(2)}, u32[]{:S(2)}) collective-permute-start(bf16[264,256]{1,0:T(8,128)(2,1)S(1)} %convert_element_type.25), channel_id=1, source_target_pairs={{0,2},{2,4},{4,6},{6,8},{8,10},{10,12},{12,14},{14,16},{16,18},{18... | collective-permute-start | bytes 405512 | tf_op jit(solution)/shard_map/ppermute | solution.py:23
  68.5 0.0 collective-permute-done.1
  68.6 1.0 collective-permute-done
  69.5 0.1 fusion.1
  69.6 1.3 collective-permute-start.3
  70.9 4.6 %collective-permute-start.2 = (bf16[264,256]{1,0:T(8,128)(2,1)S(1)}, bf16[264,256]{1,0:T(8,128)(2,1)S(1)}, u32[]{:S(2)}, u32[]{:S(2)}) collective-permute-start(bf16[264,256]{1,0:T(8,128)(2,1)S(1)} %fusion.1), channel_id=1, source_target_pairs={{0,1},{2,3},{4,5},{6,7},{8,9},{10,11},{12,13},{14,15},{16,17},{18,... | collective-permute-start | bytes 405512 | tf_op jit(solution)/shard_map/ppermute | solution.py:23
  75.4 1.2 collective-permute-done.3
  76.6 1.7 %collective-permute-done.2 = bf16[264,256]{1,0:T(8,128)(2,1)S(1)} collective-permute-done((bf16[264,256]{1,0:T(8,128)(2,1)S(1)}, bf16[264,256]{1,0:T(8,128)(2,1)S(1)}, u32[]{:S(2)}, u32[]{:S(2)}) %collective-permute-start.2) | collective-permute-done | bytes 135200 | tf_op jit(solution)/shard_map/ppermute | solution.py:23
  78.4 0.1 multiply_add_fusion.gram_ref
  78.5 59.5 %analyse.1 = bf16[256,4096]{1,0:T(8,128)(2,1)S(1)} custom-call(f32[264,256]{1,0:T(8,128)S(1)} %multiply_add_fusion.gram_ref, bf16[16,16,16,256]{3,2,1,0:T(8,128)(2,1)} %copy-done.3, bf16[256,256]{1,0:T(8,128)(2,1)S(1)} %fusion.swap_ref, f32[16,1,4096]{2,1,0:T(1,128)S(1)} %broadcast_in_dim.3.d_ref), custom_call_target="tpu_custom_call" | custom-call | flops 3556769792 | bytes 2760704 | tf_op jit(solution)/shard_map/analyse/pallas_call | solution.py:417
  138.0 1.3 copy.7
  (4 shorter events, 0.0 us)
Async XLA Ops:
  1.5 0.7 copy-start
  2.2 0.7 copy-start.1
  2.9 0.7 copy-start.2
  62.9 1.3 copy-start.3
  64.2 4.3 %collective-permute-start.1 = (bf16[264,256]{1,0:T(8,128)(2,1)S(1)}, bf16[264,256]{1,0:T(8,128)(2,1)S(1)}, u32[]{:S(2)}, u32[]{:S(2)}) collective-permute-start(bf16[264,256]{1,0:T(8,128)(2,1)S(1)} %convert_element_type.25), channel_id=1, source_target_pairs={{2,0},{4,2},{6,4},{8,6},{10,8},{12,10},{14,12},{16,14},{18,16},{20... | collective-permute-start | bytes 405512 | tf_op jit(solution)/shard_map/ppermute | solution.py:23
  65.5 4.0 %collective-permute-start = (bf16[264,256]{1,0:T(8,128)(2,1)S(1)}, bf16[264,256]{1,0:T(8,128)(2,1)S(1)}, u32[]{:S(2)}, u32[]{:S(2)}) collective-permute-start(bf16[264,256]{1,0:T(8,128)(2,1)S(1)} %convert_element_type.25), channel_id=1, source_target_pairs={{0,2},{2,4},{4,6},{6,8},{8,10},{10,12},{12,14},{14,16},{16,18},{18... | collective-permute-start | bytes 405512 | tf_op jit(solution)/shard_map/ppermute | solution.py:23
  69.6 7.1 %collective-permute-start.3 = (bf16[264,256]{1,0:T(8,128)(2,1)S(1)}, bf16[264,256]{1,0:T(8,128)(2,1)S(1)}, u32[]{:S(2)}, u32[]{:S(2)}) collective-permute-start(bf16[264,256]{1,0:T(8,128)(2,1)S(1)} %fusion.1), channel_id=1, source_target_pairs={{1,0},{3,2},{5,4},{7,6},{9,8},{11,10},{13,12},{15,14},{17,16},{19,... | collective-permute-start | bytes 405512 | tf_op jit(solution)/shard_map/ppermute | solution.py:23
  70.9 7.5 %collective-permute-start.2 = (bf16[264,256]{1,0:T(8,128)(2,1)S(1)}, bf16[264,256]{1,0:T(8,128)(2,1)S(1)}, u32[]{:S(2)}, u32[]{:S(2)}) collective-permute-start(bf16[264,256]{1,0:T(8,128)(2,1)S(1)} %fusion.1), channel_id=1, source_target_pairs={{0,1},{2,3},{4,5},{6,7},{8,9},{10,11},{12,13},{14,15},{16,17},{18,... | collective-permute-start | bytes 405512 | tf_op jit(solution)/shard_map/ppermute | solution.py:23

commit v3 on v2

v3 whole, which is shorter than its diff:
```python
import functools
import math

import jax
import jax.numpy as jnp
import numpy as np
from jax import lax
from jax.experimental import pallas as pl
from jax.experimental.pallas import tpu as pltpu
from jax.sharding import PartitionSpec as P

ITERS = 10
PAD = 128
F32 = jnp.float32
BF16 = jnp.bfloat16
MESH = pl.DeviceIdType.MESH
VMEM = pl.BlockSpec(memory_space=pltpu.VMEM)


def swap_matrix(outer, inner):
    row = np.arange(outer * inner)
    source = (row % inner) * outer + row // inner
    return jnp.asarray(source[:, None] == row[None, :], BF16)


def merged(block):
    a, m, c = block.shape
    if m % 16 == 0:
        return block.reshape(a * m, c)
    return block.astype(F32).reshape(a * m, c).astype(BF16)


def halves(value):
    high = value.astype(BF16)
    return high, (value - high.astype(F32)).astype(BF16)


def dot1(a, b):
    return jnp.dot(a, b, preferred_element_type=F32)


def dot3(a, b):
    ah, al = a
    bh, bl = b
    return dot1(ah, bh) + (dot1(ah, bl) + dot1(al, bh))


def step(src, row, diffusion, at, cols):
    lo = PAD + at
    mid = src[row, :, lo : lo + cols]
    around = (
        src[row - 1, :, lo : lo + cols]
        + src[row + 1, :, lo : lo + cols]
        + src[row, :, lo - 1 : lo - 1 + cols]
        + src[row, :, lo + 1 : lo + 1 + cols]
    )
    return mid + diffusion * (around - 4.0 * mid)


def clear_pads(buf, width):
    rows, m, _ = buf.shape
    buf[:, :, :PAD] = jnp.zeros((rows, m, PAD), F32)
    buf[:, :, PAD + width :] = jnp.zeros((rows, m, PAD), F32)


class Peers:
    def __init__(self, n, spaces):
        self.n = n
        self.me = lax.axis_index("mem")
        self.space = lax.axis_index("space")
        self.has_low = self.space > 0
        self.has_high = self.space < spaces - 1
        self.order = []
        for k in reversed(range(1, n)):
            peer, bit = self.me, 1
            while bit < n:
                if k & bit:
                    peer = peer + bit * (1 - 2 * ((self.me // bit) % 2))
                bit *= 2
            self.order.append(peer)

    def sides(self):
        return ((self.has_low, self.space - 1), (self.has_high, self.space + 1))

    def greet(self):
        barrier = pltpu.get_barrier_semaphore()
        for peer in self.order:
            pl.semaphore_signal(barrier, inc=1, device_id={"mem": peer}, device_id_type=MESH)
        for has, other in self.sides():

            @pl.when(has)
            def _():
                pl.semaphore_signal(barrier, inc=1, device_id={"space": other}, device_id_type=MESH)

    def meet(self):
        barrier = pltpu.get_barrier_semaphore()
        beside = self.has_low.astype(jnp.int32) + self.has_high.astype(jnp.int32)
        pl.semaphore_wait(barrier, self.n - 1 + beside)


class Blocks:
    def __init__(self, peers, src, dst, groups, send, recv):
        self.peers, self.src, self.dst = peers, src, dst
        self.groups, self.sems = groups, (send, recv)

    def copy(self, g, i, slot):
        first, last = self.groups[g]
        peer = self.peers.order[i]
        send, recv = self.sems
        return pltpu.make_async_remote_copy(
            src_ref=self.src.at[peer, first:last],
            dst_ref=self.dst.at[slot, first:last],
            send_sem=send.at[g, i],
            recv_sem=recv.at[g, i],
            device_id={"mem": peer},
            device_id_type=MESH,
        )

    def start(self, g):
        for i in range(len(self.peers.order)):
            self.copy(g, i, self.peers.me).start()
        first, last = self.groups[g]
        me = self.peers.me
        self.dst[me, first:last] = self.src[me, first:last]

    def arrive(self, g):
        for i in range(len(self.peers.order)):
            self.copy(g, i, self.peers.order[i]).wait_recv()

    def finish(self):
        for g in range(len(self.groups)):
            for i in range(len(self.peers.order)):
                self.copy(g, i, self.peers.me).wait_send()


class Rows:
    def __init__(self, peers, src, dst, send, recv):
        self.peers, self.src, self.dst = peers, src, dst
        self.send, self.recv = send, recv

    def copy(self, i, slot):
        peer = self.peers.order[i]
        return pltpu.make_async_remote_copy(
            src_ref=self.src(peer),
            dst_ref=self.dst.at[slot],
            send_sem=self.send.at[i],
            recv_sem=self.recv.at[i],
            device_id={"mem": peer},
            device_id_type=MESH,
        )

    def start(self):
        for i in range(len(self.peers.order)):
            self.copy(i, self.peers.me).start()

    def arrive(self):
        for i in range(len(self.peers.order)):
            self.copy(i, self.peers.order[i]).wait_recv()

    def finish(self):
        for i in range(len(self.peers.order)):
            self.copy(i, self.peers.me).wait_send()


def beside(src, dst, sems, slot, other):
    send, recv = sems
    return pltpu.make_async_remote_copy(
        src_ref=src,
        dst_ref=dst,
        send_sem=send.at[slot],
        recv_sem=recv.at[slot],
        device_id={"space": other},
        device_id_type=MESH,
    )


def cut(first, last, parts):
    size = -(-(last - first) // parts)
    return [(a, min(a + size, last)) for a in range(first, last, size)]


def transform_of(gram, vector, members):
    identity = (
        lax.broadcasted_iota(jnp.int32, (members, members), 0)
        == lax.broadcasted_iota(jnp.int32, (members, members), 1)
    ).astype(F32)
    system = gram + (members - 1.0) * identity
    frob = jnp.sqrt(jnp.sum(jnp.sum(system * system, axis=1, keepdims=True), axis=0, keepdims=True))
    root_part = system / frob
    factor = 1.5 * identity - 0.5 * root_part
    root_part = dot3(halves(root_part), halves(factor))
    inverse_part = factor
    for index in range(1, ITERS):
        r, z = halves(root_part), halves(inverse_part)
        f = halves(1.5 * identity - 0.5 * dot3(z, r))
        if index < ITERS - 1:
            root_part = dot3(r, f)
        inverse_part = dot3(f, z)
    inverse_root = inverse_part / jnp.sqrt(frob)
    z = halves(inverse_root)
    weights = dot3(halves(dot3(halves(vector), z)), z)[0:1, :]
    return (math.sqrt(members - 1.0) * inverse_root + weights).astype(BF16)


def row_groups(rows):
    return cut(2, rows - 2, 3), [(0, 2), (rows - 2, rows)]


def cycle_kernel(
    spaces, x_ref, swap_ref, swap_back_ref, d_ref, site_ref, value_ref, weight_ref, out_ref,
    xs, v1, fresh, patch, updated, back, moved, edge_out, edge_in, d_out, d_in, last_in,
    sites, seen_out, seen, gram_out, gram_in, turned,
    send, recv, return_send, return_recv, side_send, side_recv,
    site_send, site_recv, seen_send, seen_recv, gram_send, gram_recv,
):
    patches, rows, m, cols = patch.shape
    width = patches * cols
    members = patches * m
    obs = site_ref.shape[1]
    peers = Peers(patches, spaces)
    peers.greet()
    me = peers.me
    middle, edges = row_groups(rows)
    groups = middle[:2] + edges + middle[2:]
    blocks = Blocks(peers, fresh, patch, groups, send, recv)
    returned = edges + middle
    returns = Blocks(peers, updated, back, returned, return_send, return_recv)
    site_blocks = Rows(peers, lambda peer: sites.at[me], sites, site_send, site_recv)
    seen_blocks = Rows(peers, lambda peer: seen_out.at[peer], seen, seen_send, seen_recv)
    side = (side_send, side_recv)
    sides = list(enumerate(peers.sides()))

    sites[me] = site_ref[...]
    clear_pads(xs, width)
    clear_pads(v1, width)
    d_out[0] = d_ref[0:1, :]
    d_out[1] = d_ref[rows - 1 : rows, :]
    for c in range(patches // 2):
        at = c * 2 * cols
        part = dot1(swap_ref[...], x_ref[:, at : at + 2 * cols]).reshape(rows, m, 2 * cols)
        xs[2 : rows + 2, :, PAD + at : PAD + at + 2 * cols] = part
        edge_out[0, :, :, at : at + 2 * cols] = part[:2].astype(BF16)
        edge_out[1, :, :, at : at + 2 * cols] = part[rows - 2 :].astype(BF16)

    peers.meet()

    def halo(k, other):
        return (
            beside(edge_out.at[k], edge_in.at[1 - k], side, k, other),
            beside(d_out.at[k], d_in.at[1 - k], side, 2 + k, other),
        )

    def halo_in(k, other):
        return (
            beside(edge_out.at[k], edge_in.at[k], side, 1 - k, other),
            beside(d_out.at[k], d_in.at[k], side, 3 - k, other),
        )

    for k, (has, other) in sides:

        @pl.when(has)
        def _():
            for copy in halo(k, other):
                copy.start()

    site_blocks.start()

    def first_step(r, d_row):
        for q in range(patches):
            at = q * cols
            v1[r, :, PAD + at : PAD + at + cols] = step(xs, r, d_row(at), at, cols)

    def second_step(r):
        for q in range(patches):
            at = q * cols
            d_row = d_ref[pl.ds(r - 2, 1), at : at + cols]
            fresh[q, r - 2] = step(v1, r, d_row, at, cols).astype(BF16)

    done = 3
    for g, (first, last) in enumerate(middle):

        @pl.loop(done, last + 3)
        def _(r):
            first_step(r, lambda at: d_ref[pl.ds(r - 2, 1), at : at + cols])

        done = last + 3

        @pl.loop(first + 2, last + 2)
        def _(r):
            second_step(r)

        if g == 0:
            blocks.start(0)

    for k, (has, other) in sides:
        row = 0 if k == 0 else rows + 2

        @pl.when(has)
        def _():
            for copy in halo_in(k, other):
                copy.wait_recv()
            xs[row : row + 2, :, PAD : PAD + width] = edge_in[k].astype(F32)

        @pl.when(jnp.logical_not(has))
        def _():
            xs[row : row + 2, :, PAD : PAD + width] = jnp.zeros((2, m, width), F32)
            d_in[k] = jnp.zeros((1, width), F32)

        outer, inner = (1, 2) if k == 0 else (rows + 2, rows + 1)
        first_step(outer, lambda at: d_in[k, :, at : at + cols])
        first_step(inner, lambda at: d_ref[inner - 2 : inner - 1, at : at + cols])

        @pl.loop(edges[k][0] + 2, edges[k][1] + 2)
        def _(r):
            second_step(r)

    site_blocks.arrive()

    @pl.loop(0, patches)
    def _(q):
        lanes = 128
        at = [
            jnp.broadcast_to(sites[q, :, o * lanes : (o + 1) * lanes], (m, lanes))
            for o in range(obs // lanes)
        ]
        lane = [v % lanes for v in at]
        tile = [v // lanes for v in at]
        picked = [jnp.zeros((m, lanes), F32) for _ in at]
        for r in range(rows):
            for h in range(cols // lanes):
                cells = fresh[q, r, :, h * lanes : (h + 1) * lanes].astype(F32)
                number = r * (cols // lanes) + h
                for o in range(len(at)):
                    got = jnp.take_along_axis(cells, lane[o], axis=1, mode="promise_in_bounds")
                    picked[o] = jnp.where(tile[o] == number, got, picked[o])
        for o in range(len(at)):
            seen_out[q, :, o * lanes : (o + 1) * lanes] = picked[o].astype(BF16)

    seen_blocks.start()
    seen[me] = seen_out[me]
    blocks.start(1)
    seen_blocks.arrive()

    observed = merged(seen[...]).astype(F32)
    obs_mean = jnp.sum(observed, axis=0, keepdims=True) * (1.0 / members)
    root = jnp.sqrt(weight_ref[...])
    spread = ((observed - obs_mean) * root).astype(BF16)
    innovation = ((value_ref[...] - obs_mean) * root).astype(BF16)
    contract = (((1,), (1,)), ((), ()))
    gram_out[0, 0:members, :] = lax.dot_general(
        spread, spread, contract, preferred_element_type=F32
    )
    wide = jnp.broadcast_to(innovation.astype(F32), (8, obs)).astype(BF16)
    gram_out[0, members : members + 8, :] = lax.dot_general(
        wide, spread, contract, preferred_element_type=F32
    )

    def to_beside(stage, k, axis, other):
        return pltpu.make_async_remote_copy(
            src_ref=gram_out.at[stage],
            dst_ref=gram_in.at[stage, 1 - k],
            send_sem=gram_send.at[stage, k],
            recv_sem=gram_recv.at[stage, 1 - k],
            device_id={axis: other},
            device_id_type=MESH,
        )

    def from_beside(stage, k, axis, other):
        return pltpu.make_async_remote_copy(
            src_ref=gram_out.at[stage],
            dst_ref=gram_in.at[stage, k],
            send_sem=gram_send.at[stage, k],
            recv_sem=gram_recv.at[stage, k],
            device_id={axis: other},
            device_id_type=MESH,
        )

    def gram_send_all(stage, axis, pairs):
        for k, (has, other) in enumerate(pairs):

            @pl.when(has)
            def _():
                to_beside(stage, k, axis, other).start()

            @pl.when(jnp.logical_not(has))
            def _():
                gram_in[stage, k] = jnp.zeros((members + 8, members), F32)

    def gram_sum(stage, axis, pairs):
        for k, (has, other) in enumerate(pairs):

            @pl.when(has)
            def _():
                from_beside(stage, k, axis, other).wait_recv()

        return gram_out[stage] + 0.5 * (gram_in[stage, 0] + gram_in[stage, 1])

    along = ((me > 0, me - 1), (me < patches - 1, me + 1))
    gram_send_all(0, "mem", along)
    for g in range(2, len(groups)):
        blocks.start(g)
    gram_out[1] = gram_sum(0, "mem", along)
    gram_send_all(1, "space", peers.sides())
    gram_out[2] = gram_sum(1, "space", peers.sides())
    turned[...] = transform_of(gram_out[2, 0:members], gram_out[2, members:], members)

    arrived = set()
    for g, (first, last) in enumerate(returned):
        index = groups.index((first, last))
        for earlier in range(index + 1):
            if earlier not in arrived:
                blocks.arrive(earlier)
                arrived.add(earlier)

        @pl.loop(first, last)
        def _(r):
            cells = merged(patch[:, r]).astype(F32)
            mean = jnp.sum(cells, axis=0, keepdims=True) * (1.0 / members)
            result = mean + dot1(turned[...], (cells - mean).astype(BF16))
            updated[:, r] = result.reshape(patches, m, cols).astype(BF16)

        returns.start(g)

    def last_halo(k, other):
        row = 0 if k == 0 else rows - 1
        return beside(back.at[:, row], last_in.at[1 - k], side, 4 + k, other)

    def last_halo_in(k, other):
        return beside(back.at[:, 0], last_in.at[k], side, 5 - k, other)

    def take(r):
        for q in range(patches):
            xs[r + 1, :, PAD + q * cols : PAD + (q + 1) * cols] = back[q, r].astype(F32)

    def last_step(r, d_row):
        for q in range(patches):
            at = q * cols
            moved[r, :, at : at + cols] = step(xs, r + 1, d_row(at), at, cols).astype(BF16)

    for k, (has, other) in sides:
        returns.arrive(k)

        @pl.when(has)
        def _():
            last_halo(k, other).start()

        @pl.loop(*edges[k])
        def _(r):
            take(r)

    done = 1
    for g in range(2, len(returned)):
        first, last = returned[g]
        returns.arrive(g)

        @pl.loop(first, last)
        def _(r):
            take(r)

        upto = rows - 1 if g == len(returned) - 1 else last - 1

        @pl.loop(done, upto)
        def _(r):
            last_step(r, lambda at: d_ref[pl.ds(r, 1), at : at + cols])

        done = upto
        if g == 2:
            for k, (has, other) in sides:
                row = 0 if k == 0 else rows + 1

                @pl.when(has)
                def _():
                    last_halo_in(k, other).wait_recv()
                    for q in range(patches):
                        xs[row, :, PAD + q * cols : PAD + (q + 1) * cols] = last_in[k, q].astype(F32)

                @pl.when(jnp.logical_not(has))
                def _():
                    xs[row, :, PAD : PAD + width] = jnp.zeros((m, width), F32)

                r = 0 if k == 0 else rows - 1
                last_step(r, lambda at: d_ref[r : r + 1, at : at + cols])

    for c in range(patches // 2):
        at = c * 2 * cols
        part = merged(moved[:, :, at : at + 2 * cols])
        out_ref[:, at : at + 2 * cols] = dot1(swap_back_ref[...], part).astype(BF16)

    for sent in (blocks, returns, site_blocks, seen_blocks):
        sent.finish()
    for k, (has, other) in sides:

        @pl.when(has)
        def _():
            for copy in (*halo(k, other), last_halo(k, other)):
                copy.wait_send()

    for stage, axis, pairs in ((0, "mem", along), (1, "space", peers.sides())):
        for k, (has, other) in enumerate(pairs):

            @pl.when(has)
            def _():
                to_beside(stage, k, axis, other).wait_send()


def body(prior, diffusivity, site, quantities, weightings):
    m, rows, width = prior.shape
    patches = lax.axis_size("mem")
    spaces = lax.axis_size("space")
    cols = width // patches
    members = m * patches
    obs = site.shape[-1]
    padded = width + 2 * PAD
    dma = pltpu.SemaphoreType.DMA
    many = sum(map(len, row_groups(rows)))
    others = patches - 1
    args = (
        prior.reshape(m * rows, width),
        swap_matrix(rows, m),
        swap_matrix(m, rows),
        diffusivity,
        site[0],
        quantities[0],
        weightings[0],
    )
    bulk = pltpu.VMEM((patches, rows, m, cols), BF16)
    out = pl.pallas_call(
        functools.partial(cycle_kernel, spaces),
        out_shape=jax.ShapeDtypeStruct((m * rows, width), BF16),
        in_specs=[VMEM] * len(args),
        out_specs=VMEM,
        scratch_shapes=[
            pltpu.VMEM((rows + 4, m, padded), F32),
            pltpu.VMEM((rows + 4, m, padded), F32),
            bulk,
            bulk,
            bulk,
            bulk,
            pltpu.VMEM((rows, m, width), BF16),
            pltpu.VMEM((2, 2, m, width), BF16),
            pltpu.VMEM((2, 2, m, width), BF16),
            pltpu.VMEM((2, 1, width), F32),
            pltpu.VMEM((2, 1, width), F32),
            pltpu.VMEM((2, patches, m, cols), BF16),
            pltpu.VMEM((patches, 1, obs), jnp.int32),
            pltpu.VMEM((patches, m, obs), BF16),
            pltpu.VMEM((patches, m, obs), BF16),
            pltpu.VMEM((3, members + 8, members), F32),
            pltpu.VMEM((2, 2, members + 8, members), F32),
            pltpu.VMEM((members, members), BF16),
            *[dma((many, others))] * 4,
            dma((6,)),
            dma((6,)),
            *[dma((others,))] * 4,
            dma((2, 2)),
            dma((2, 2)),
        ],
        compiler_params=pltpu.CompilerParams(
            vmem_limit_bytes=58 * 2**20, collective_id=0, has_side_effects=True
        ),
        name="cycle",
    )(*args)
    return out.reshape(m, rows, width)


def solution(mesh):
    return jax.shard_map(
        body,
        mesh=mesh,
        in_specs=(
            P("mem", "space", None),
            P("space", None),
            P("space", "mem", None),
            P("space", "mem", None),
            P("space", "mem", None),
        ),
        out_specs=P("mem", "space", None),
        check_vma=False,
    )
```

time: 140 us -> 124 us (0.89)
  starting transfers between devices: 10.2 us -> 0 us
  waiting for transfers between devices: 3.92 us -> 0 us
  local copies, waits for them, and re-layouts: 5.89 us -> 3.13 us
  Pallas kernels: 119 us -> 121 us
    ppermute x4 -> x0, starting transfers between devices: 10.2 us -> none  [the longest x2 7.6 us: exchange(): lax.ppermute(high_edge, axis, forward)]
    ppermute x4 -> x0, waiting for transfers between devices: 3.92 us -> none  [the longest x2 2.7 us: exchange(): lax.ppermute(high_edge, axis, forward)]
    pallas_call x2 -> x1, Pallas kernels: 119 us -> 121 us  [body(): pl.pallas_call(functools.partial(cycle_kernel, spaces), out_shape=jax.Sha...]
    unnamed x9 -> x1, local copies, waits for them, and re-layouts: 4.67 us -> 3.13 us
  transfers between devices with their start and end apart: 4 -> 0, of which waited for: 3 -> 0; matrix products, arithmetic and copies ran while one was open for 0% -> 0% of each run, Pallas kernels for 0% -> 0%
where the time goes in v3:
time: 124 us
  Pallas kernels  121 us (98%)
  local copies, waits for them, and re-layouts  3.13 us (3%)
    pallas_call x1, Pallas kernels, body(): pl.pallas_call(functools.partial(cycle_kernel, spaces), out_shape=jax.Sha...  121 us
    unnamed x1, local copies, waits for them, and re-layouts  3.13 us

profile of v3, /device:TPU:0, one launch (start us, length us, event | category | flops | bytes accessed | tf_op | source)
XLA Modules:
  0.0 123.9 jit_solution(15524971611818696315)
XLA Ops:
  0.0 120.8 %cycle.1 = bf16[256,4096]{1,0:T(8,128)(2,1)} custom-call(bf16[256,4096]{1,0:T(8,128)(2,1)} %bitcast.6, bf16[256,256]{1,0:T(8,128)(2,1)} %constant.2.clone.swap_ref.swap_back_ref, bf16[256,256]{1,0:T(8,128)(2,1)} %constant.2.clone.swap_ref.swap_back_ref, f32[16,4096]{1,0:T(8,128)} %d_ref.1, s32[1,512]{1,0:T(1,128)} %bitcast.7, f32[1,512]{1,0:T(1,128)} %bitcast.8, ...), custom_call_target="tpu_custom_call" | custom-call | tf_op jit(solution)/shard_map/cycle/pallas_call | solution.py:527
  120.8 3.1 %copy.9 = bf16[16,16,4096]{2,1,0:T(8,128)(2,1)} copy(bf16[16,16,4096]{2,1,0:T(8,128)(2,1)} %bitcast.5) | data formatting | bytes 4194304

commit v4 on v3

--- a/solution.py
+++ b/solution.py
@@ -116,8 +116,9 @@
             device_id_type=MESH,
         )
 
-    def start(self, g):
-        for i in range(len(self.peers.order)):
+    def start(self, g, near_first=False):
+        order = range(len(self.peers.order))
+        for i in reversed(order) if near_first else order:
             self.copy(g, i, self.peers.me).start()
         first, last = self.groups[g]
         me = self.peers.me
@@ -206,9 +207,18 @@
     return cut(2, rows - 2, 3), [(0, 2), (rows - 2, rows)]
 
 
+def swap_kernel(swap_ref, moved_ref, out_ref):
+    out_ref[...] = dot1(swap_ref[...], merged(moved_ref[...])).astype(BF16)
+
+
+def return_groups(rows):
+    middle, edges = row_groups(rows)
+    return edges + middle[:-1] + cut(*middle[-1], 2)
+
+
 def cycle_kernel(
-    spaces, x_ref, swap_ref, swap_back_ref, d_ref, site_ref, value_ref, weight_ref, out_ref,
-    xs, v1, fresh, patch, updated, back, moved, edge_out, edge_in, d_out, d_in, last_in,
+    spaces, x_ref, swap_ref, d_ref, site_ref, value_ref, weight_ref, moved,
+    xs, v1, fresh, patch, updated, back, edge_out, edge_in, d_out, d_in, last_in,
     sites, seen_out, seen, gram_out, gram_in, turned,
     send, recv, return_send, return_recv, side_send, side_recv,
     site_send, site_recv, seen_send, seen_recv, gram_send, gram_recv,
@@ -223,7 +233,7 @@
     middle, edges = row_groups(rows)
     groups = middle[:2] + edges + middle[2:]
     blocks = Blocks(peers, fresh, patch, groups, send, recv)
-    returned = edges + middle
+    returned = return_groups(rows)
     returns = Blocks(peers, updated, back, returned, return_send, return_recv)
     site_blocks = Rows(peers, lambda peer: sites.at[me], sites, site_send, site_recv)
     seen_blocks = Rows(peers, lambda peer: seen_out.at[peer], seen, seen_send, seen_recv)
@@ -406,7 +416,7 @@
 
     arrived = set()
     for g, (first, last) in enumerate(returned):
-        index = groups.index((first, last))
+        index = max(i for i, (low, high) in enumerate(groups) if low < last and high > first)
         for earlier in range(index + 1):
             if earlier not in arrived:
                 blocks.arrive(earlier)
@@ -419,7 +429,7 @@
             result = mean + dot1(turned[...], (cells - mean).astype(BF16))
             updated[:, r] = result.reshape(patches, m, cols).astype(BF16)
 
-        returns.start(g)
+        returns.start(g, near_first=g == len(returned) - 1)
 
     def last_halo(k, other):
         row = 0 if k == 0 else rows - 1
@@ -480,11 +490,6 @@
 
                 r = 0 if k == 0 else rows - 1
                 last_step(r, lambda at: d_ref[r : r + 1, at : at + cols])
-
-    for c in range(patches // 2):
-        at = c * 2 * cols
-        part = merged(moved[:, :, at : at + 2 * cols])
-        out_ref[:, at : at + 2 * cols] = dot1(swap_back_ref[...], part).astype(BF16)
 
     for sent in (blocks, returns, site_blocks, seen_blocks):
         sent.finish()
@@ -517,16 +522,15 @@
     args = (
         prior.reshape(m * rows, width),
         swap_matrix(rows, m),
-        swap_matrix(m, rows),
         diffusivity,
         site[0],
         quantities[0],
         weightings[0],
     )
     bulk = pltpu.VMEM((patches, rows, m, cols), BF16)
-    out = pl.pallas_call(
+    moved = pl.pallas_call(
         functools.partial(cycle_kernel, spaces),
-        out_shape=jax.ShapeDtypeStruct((m * rows, width), BF16),
+        out_shape=jax.ShapeDtypeStruct((rows, m, width), BF16),
         in_specs=[VMEM] * len(args),
         out_specs=VMEM,
         scratch_shapes=[
@@ -536,7 +540,6 @@
             bulk,
             bulk,
             bulk,
-            pltpu.VMEM((rows, m, width), BF16),
             pltpu.VMEM((2, 2, m, width), BF16),
             pltpu.VMEM((2, 2, m, width), BF16),
             pltpu.VMEM((2, 1, width), F32),
@@ -548,7 +551,8 @@
             pltpu.VMEM((3, members + 8, members), F32),
             pltpu.VMEM((2, 2, members + 8, members), F32),
             pltpu.VMEM((members, members), BF16),
-            *[dma((many, others))] * 4,
+            *[dma((many, others))] * 2,
+            *[dma((len(return_groups(rows)), others))] * 2,
             dma((6,)),
             dma((6,)),
             *[dma((others,))] * 4,
@@ -560,6 +564,18 @@
         ),
         name="cycle",
     )(*args)
+    size, lanes = m * rows, width // 4
+    out = pl.pallas_call(
+        swap_kernel,
+        out_shape=jax.ShapeDtypeStruct((size, width), BF16),
+        grid=(4,),
+        in_specs=[
+            pl.BlockSpec((size, size), lambda c: (0, 0)),
+            pl.BlockSpec((rows, m, lanes), lambda c: (0, 0, c)),
+        ],
+        out_specs=pl.BlockSpec((size, lanes), lambda c: (0, c)),
+        name="swap",
+    )(swap_matrix(m, rows), moved)
     return out.reshape(m, rows, width)
 
 

time: 124 us -> 123 us (level)
  local copies, waits for them, and re-layouts: 3.13 us -> 0 us
  Pallas kernels: 121 us -> 123 us
    pallas_call x0 -> x1, Pallas kernels: none -> 4.35 us  [body(): pl.pallas_call(swap_kernel, out_shape=jax.ShapeDtypeStruct((size, width),...]
    unnamed x1 -> x0, local copies, waits for them, and re-layouts: 3.13 us -> none
    pallas_call x1, Pallas kernels: 121 us -> 119 us  [body(): pl.pallas_call(functools.partial(cycle_kernel, spaces), out_shape=jax.Sha...]
where the time goes in v4:
time: 123 us
  Pallas kernels  123 us (100%)
    pallas_call x1, Pallas kernels, body(): pl.pallas_call(functools.partial(cycle_kernel, spaces), out_shape=jax.Sha...  119 us
    pallas_call x1, Pallas kernels, body(): pl.pallas_call(swap_kernel, out_shape=jax.ShapeDtypeStruct((size, width),...  4.35 us

profile of v4, /device:TPU:0, one launch (start us, length us, event | category | flops | bytes accessed | tf_op | source)
XLA Modules:
  0.0 123.1 jit_solution(8226786405347051610)
XLA Ops:
  0.0 118.7 %cycle.1.moved_ref = bf16[16,16,4096]{2,1,0:T(8,128)(2,1)} custom-call(bf16[256,4096]{1,0:T(8,128)(2,1)} %bitcast.5, bf16[256,256]{1,0:T(8,128)(2,1)} %constant.2.clone.swap_ref, f32[16,4096]{1,0:T(8,128)} %d_ref.1, s32[1,512]{1,0:T(1,128)} %bitcast.6, f32[1,512]{1,0:T(1,128)} %bitcast.7, f32[1,512]{1,0:T(1,128)} %bitcast.8), custom_call_target="tpu_custom_call" | custom-call | tf_op jit(solution)/shard_map/cycle/pallas_call | solution.py:531
  118.7 4.4 %swap.1 = bf16[256,4096]{1,0:T(8,128)(2,1)} custom-call(bf16[256,256]{1,0:T(8,128)(2,1)} %constant.2.clone.swap_ref, bf16[16,16,4096]{2,1,0:T(8,128)(2,1)} %cycle.1.moved_ref), custom_call_target="tpu_custom_call" | custom-call | tf_op jit(solution)/shard_map/swap/pallas_call | solution.py:568

commit v5 on v4

--- a/solution.py
+++ b/solution.py
@@ -204,7 +204,7 @@
 
 
 def row_groups(rows):
-    return cut(2, rows - 2, 3), [(0, 2), (rows - 2, rows)]
+    return cut(2, rows - 2, 4), [(0, 2), (rows - 2, rows)]
 
 
 def swap_kernel(swap_ref, moved_ref, out_ref):
@@ -231,7 +231,7 @@
     peers.greet()
     me = peers.me
     middle, edges = row_groups(rows)
-    groups = middle[:2] + edges + middle[2:]
+    groups = middle[:3] + edges + middle[3:]
     blocks = Blocks(peers, fresh, patch, groups, send, recv)
     returned = return_groups(rows)
     returns = Blocks(peers, updated, back, returned, return_send, return_recv)
@@ -299,8 +299,8 @@
         def _(r):
             second_step(r)
 
-        if g == 0:
-            blocks.start(0)
+        if g < 2:
+            blocks.start(g)
 
     for k, (has, other) in sides:
         row = 0 if k == 0 else rows + 2
@@ -348,7 +348,7 @@
 
     seen_blocks.start()
     seen[me] = seen_out[me]
-    blocks.start(1)
+    blocks.start(2)
     seen_blocks.arrive()
 
     observed = merged(seen[...]).astype(F32)
@@ -407,7 +407,7 @@
 
     along = ((me > 0, me - 1), (me < patches - 1, me + 1))
     gram_send_all(0, "mem", along)
-    for g in range(2, len(groups)):
+    for g in range(3, len(groups)):
         blocks.start(g)
     gram_out[1] = gram_sum(0, "mem", along)
     gram_send_all(1, "space", peers.sides())
@@ -560,7 +560,7 @@
             dma((2, 2)),
         ],
         compiler_params=pltpu.CompilerParams(
-            vmem_limit_bytes=58 * 2**20, collective_id=0, has_side_effects=True
+            vmem_limit_bytes=36 * 2**20, collective_id=0, has_side_effects=True
         ),
         name="cycle",
     )(*args)
@@ -574,6 +574,7 @@
             pl.BlockSpec((rows, m, lanes), lambda c: (0, 0, c)),
         ],
         out_specs=pl.BlockSpec((size, lanes), lambda c: (0, c)),
+        compiler_params=pltpu.CompilerParams(vmem_limit_bytes=16 * 2**20),
         name="swap",
     )(swap_matrix(m, rows), moved)
     return out.reshape(m, rows, width)

time: 123 us -> 122 us (level)
  Pallas kernels: 123 us -> 116 us
  local copies, waits for them, and re-layouts: 0 us -> 5.49 us
    unnamed x0 -> x12, local copies, waits for them, and re-layouts: none -> 5.49 us
    pallas_call x1, Pallas kernels: 119 us -> 114 us  [body(): pl.pallas_call(functools.partial(cycle_kernel, spaces), out_shape=jax.Sha...]
    pallas_call x1, Pallas kernels: 4.35 us -> 2.64 us  [body(): pl.pallas_call(swap_kernel, out_shape=jax.ShapeDtypeStruct((size, width),...]
where the time goes in v5:
time: 122 us
  Pallas kernels  116 us (95%)
  local copies, waits for them, and re-layouts  5.49 us (4%)
    pallas_call x1, Pallas kernels, body(): pl.pallas_call(functools.partial(cycle_kernel, spaces), out_shape=jax.Sha...  114 us
    unnamed x12, local copies, waits for them, and re-layouts  5.49 us
    pallas_call x1, Pallas kernels, body(): pl.pallas_call(swap_kernel, out_shape=jax.ShapeDtypeStruct((size, width),...  2.64 us

profile of v5, /device:TPU:0, one launch (start us, length us, event | category | flops | bytes accessed | tf_op | source)
XLA Modules:
  0.0 121.7 jit_solution(1585204166861350138)
XLA Ops:
  0.0 0.0 copy-start
  0.0 1.6 %copy-done = bf16[16,16,4096]{2,1,0:T(8,128)(2,1)S(1)} copy-done((bf16[16,16,4096]{2,1,0:T(8,128)(2,1)S(1)}, bf16[16,16,4096]{2,1,0:T(8,128)(2,1)}, u32[]{:S(2)}) %copy-start) | copy-done | bytes 2097176
  1.6 0.0 copy-start.1
  1.6 0.9 copy-done.1
  2.5 0.0 copy-start.2
  2.5 0.9 copy-done.2
  3.4 0.0 copy-start.3
  3.4 0.7 copy-done.3
  4.1 0.0 copy-start.4
  4.1 0.7 copy-done.4
  4.8 0.0 copy-start.5
  4.8 0.7 copy-done.5
  5.5 113.6 %cycle.1.moved_ref = bf16[16,16,4096]{2,1,0:T(8,128)(2,1)S(1)} custom-call(bf16[256,4096]{1,0:T(8,128)(2,1)S(1)} %bitcast.5, bf16[256,256]{1,0:T(8,128)(2,1)S(1)} %copy-done.1, f32[16,4096]{1,0:T(8,128)S(1)} %copy-done.2, s32[1,512]{1,0:T(1,128)S(1)} %bitcast.6, f32[1,512]{1,0:T(1,128)S(1)} %bitcast.7, f32[1,512]{1,0:T(1,128)S(1)} %bitcast.8), custom_call_target="tpu_custom_call" | custom-call | tf_op jit(solution)/shard_map/cycle/pallas_call | solution.py:531
  119.1 2.6 %swap.1 = bf16[256,4096]{1,0:T(8,128)(2,1)} custom-call(bf16[256,256]{1,0:T(8,128)(2,1)S(1)} %copy-done.1, bf16[16,16,4096]{2,1,0:T(8,128)(2,1)S(1)} %cycle.1.moved_ref), custom_call_target="tpu_custom_call" | custom-call | tf_op jit(solution)/shard_map/swap/pallas_call | solution.py:568
Async XLA Ops:
  0.0 1.6 %copy-start = (bf16[16,16,4096]{2,1,0:T(8,128)(2,1)S(1)}, bf16[16,16,4096]{2,1,0:T(8,128)(2,1)}, u32[]{:S(2)}) copy-start(bf16[16,16,4096]{2,1,0:T(8,128)(2,1)} %param.7) | copy-start | bytes 6291460
  1.6 0.9 copy-start.1
  2.5 0.9 copy-start.2
  3.4 0.7 copy-start.3
  4.1 0.7 copy-start.4
  4.8 0.7 copy-start.5
